TPU v7x, 128 devices: a whole 4x4x4 slice. The times are simulated.
128 devices in a mesh: sec: 4 (over y), row: 8 (over x, core), col: 4 (over z).
Axes of the slice: x: 4, y: 4, z: 4, core: 2. Of those that a mesh axis runs over, the one named last changes fastest.
Arguments:
- child_inv: bfloat16 [4, 4096, 4096], P('sec', 'col', 'row'), as said below
- child_low: bfloat16 [4, 2048, 4096], P('sec', 'row', 'col'), may hold values from -0.09375 to 0.09375
- parent_inv: bfloat16 [4, 6144, 3072], P('sec', 'col', 'row'), as said below
- parent_low: bfloat16 [4, 2048, 3072], P('sec', 'row', 'col'), may hold values from -0.078125 to 0.078125
- root_inv: bfloat16 [12288, 12288], P('col', ('sec', 'row')), as said below
- child_map: int32 [4, 2048], replicated, may hold values from 0 to 8191, as said below
- parent_map: int32 [2, 2048], replicated, may hold values from 0 to 12287, as said below
- child_rhs: float32 [4, 4096, 512], P('sec', 'row', 'col'), may hold values from -6 to 6
- parent_rhs: float32 [4, 3072, 512], P('sec', 'row', 'col'), may hold values from -6 to 6
- root_rhs: float32 [12288, 512], P(('sec', 'row'), 'col'), may hold values from -6 to 6
- child_back: float32 [4, 4096, 512], P('sec', 'col', 'row'), may hold values from -6 to 6
- parent_back: float32 [4, 3072, 512], P('sec', 'col', 'row'), may hold values from -6 to 6
- root_back: float32 [4, 3072, 512], P('col', ('sec', 'row')), may hold values from -6 to 6
Outputs:
- child_up: float32 [4, 4096, 512], P('sec', 'col', 'row')
- parent_up: float32 [4, 3072, 512], P('sec', 'col', 'row')
- root_up: float32 [4, 3072, 512], P('col', ('sec', 'row'))
- child_x: float32 [4, 4096, 512], P('sec', 'row', 'col')
- parent_x: float32 [4, 3072, 512], P('sec', 'row', 'col')
- root_x: float32 [12288, 512], P(('sec', 'row'), 'col')
Inputs may be any that keep to these rules, and one draw needn't show every extreme that they name: `child_inv`: zero above the diagonal of each child pivot block. `parent_inv`: the two halves side by side are zero above the diagonal. `root_inv`: zero above the diagonal. `child_map`: entries of one row are distinct; row s points into the front of parent s // 2. `parent_map`: entries of one row are distinct.
All inputs are finite; a program needn't handle non-finite values.
Results may differ from a plain program's by a relative error of at most 0.014.
Values may be sent and summed in bfloat16 or wider, within the bound.
A program may use at most 64 MiB of HBM per device.

v0:
```python
import jax
import jax.numpy as jnp
from jax import lax
from jax.sharding import PartitionSpec as P

C1 = 2048
P2 = 6144
C2 = 2048
P3 = 12288


def from_partner(x, axis, bit):
    return lax.ppermute(x, axis, [(i, i ^ 1 << bit) for i in range(lax.axis_size(axis))])


def spread_cols(block):
    return lax.all_gather(block, "col", axis=1, tiled=True)


def spread_rows(block):
    return lax.all_gather(block, "row", axis=1, tiled=True)


def sum_rows(block):
    return lax.psum_scatter(block, "row", scatter_dimension=1, tiled=True)


def sum_cols(block):
    return lax.psum_scatter(block, "col", scatter_dimension=1, tiled=True)


def pair_sums(block):
    return from_partner(block, "sec", 0)


def pair_values(block):
    return from_partner(block, "sec", 0)


def root_gather(block):
    return lax.all_gather(block, ("sec", "row"), axis=0, tiled=True)


def matmul(left, right):
    return jnp.dot(left, right, preferred_element_type=jnp.float32)


def front_slot(target, n_row):
    pivot_rows = P2 // (2 * n_row)
    cont_rows = C2 // (2 * n_row)
    stride = pivot_rows + cont_rows
    half_size = P2 // 2
    pivot_slot = (
        target // half_size * n_row + target % half_size // pivot_rows
    ) * stride + target % pivot_rows
    offset = target - P2
    cont_slot = (
        (offset % (2 * cont_rows) // cont_rows * n_row + offset // (2 * cont_rows)) * stride
        + pivot_rows
        + offset % cont_rows
    )
    return jnp.where(target < P2, pivot_slot, cont_slot)


def pair_reduce(block, pair_side):
    amount = block.shape[0] // 2
    keep = lax.dynamic_slice_in_dim(block, pair_side * amount, amount, 0)
    away = lax.dynamic_slice_in_dim(block, (1 - pair_side) * amount, amount, 0)
    return keep + pair_sums(away)


def pair_join(mine, other, pair_side):
    return jnp.where(
        pair_side == 0, jnp.concatenate([mine, other], 0), jnp.concatenate([other, mine], 0)
    )


def per_device(
    child_inv,
    child_low,
    parent_inv,
    parent_low,
    root_inv,
    child_map,
    parent_map,
    child_rhs,
    parent_rhs,
    root_rhs,
    child_back,
    parent_back,
    root_back,
):
    n_row = lax.axis_size("row")
    section = lax.axis_index("sec")
    row_id = lax.axis_index("row")
    pair_side = section % 2
    parent_id = section // 2
    pivot_rows = P2 // (2 * n_row)
    cont_rows = C2 // (2 * n_row)
    stride = pivot_rows + cont_rows
    child_tile = child_inv[0]
    partial_value = matmul(child_tile, spread_cols(child_rhs[0].astype(jnp.bfloat16)))
    child_up = sum_rows(partial_value)
    solved = spread_rows(child_up.astype(jnp.bfloat16))
    contrib = -sum_cols(matmul(child_low[0], solved))
    own_map = lax.dynamic_slice_in_dim(child_map, section, 1, 0)[0]
    child_slots = front_slot(own_map, n_row)
    local_slots = lax.dynamic_slice_in_dim(child_slots, row_id * contrib.shape[0], contrib.shape[0])
    dense = (
        jnp.zeros((2 * n_row * stride, contrib.shape[1]), jnp.float32).at[local_slots].add(contrib)
    )
    folded = lax.psum_scatter(
        dense.reshape(2, n_row * stride, contrib.shape[1]), "row", scatter_dimension=1, tiled=True
    )
    mine = lax.dynamic_index_in_dim(folded, pair_side, 0, keepdims=False)
    other = lax.dynamic_index_in_dim(folded, 1 - pair_side, 0, keepdims=False)
    front = mine + pair_sums(other)
    pivot_in = parent_rhs[0] + front[:pivot_rows]
    share = sum_rows(matmul(parent_inv[0], spread_cols(pivot_in.astype(jnp.bfloat16))))
    parent_up = pair_reduce(share, pair_side)
    update = sum_cols(matmul(parent_low[0], spread_rows(parent_up.astype(jnp.bfloat16))))
    contrib_two = front[pivot_rows:] - pair_reduce(update, pair_side)
    map_row = lax.dynamic_slice_in_dim(parent_map, parent_id, 1, 0)[0]
    mine_targets = lax.dynamic_slice_in_dim(
        map_row, row_id * 2 * cont_rows + pair_side * cont_rows, cont_rows
    )
    dense_root = (
        jnp.zeros((P3, contrib_two.shape[1]), jnp.float32).at[mine_targets].add(contrib_two)
    )
    root_front = lax.psum_scatter(
        dense_root.astype(jnp.bfloat16), ("sec", "row"), scatter_dimension=0, tiled=True
    ).astype(jnp.float32)
    root_in = root_rhs + root_front
    root_wide = spread_cols(root_in.astype(jnp.bfloat16))
    root_part = matmul(root_inv, root_wide)
    root_up = lax.psum_scatter(
        root_part.astype(jnp.bfloat16), ("sec", "row"), scatter_dimension=0, tiled=True
    ).astype(jnp.float32)
    back_wide = root_gather(root_back[0].astype(jnp.bfloat16))
    root_x = sum_cols(matmul(root_inv.T, back_wide))
    root_all = root_gather(root_x.astype(jnp.bfloat16))
    block_targets = lax.dynamic_slice_in_dim(map_row, row_id * 2 * cont_rows, 2 * cont_rows)
    picked = jnp.take(root_all, block_targets, axis=0)
    residue = parent_back[0] - sum_rows(matmul(parent_low[0].T, spread_cols(picked)))
    residue_wide = spread_rows(residue.astype(jnp.bfloat16))
    full_residue = pair_join(residue_wide, pair_values(residue_wide), pair_side)
    parent_x = sum_cols(matmul(parent_inv[0].T, full_residue))
    own_cont = lax.dynamic_slice_in_dim(picked, pair_side * cont_rows, cont_rows, 0)
    front_x = jnp.concatenate([parent_x.astype(jnp.bfloat16), own_cont], 0)
    side_rows = lax.all_gather(front_x, "row", axis=0, tiled=True)
    whole_front = pair_join(side_rows, pair_values(side_rows), pair_side)
    child_count = C1 // n_row
    row_slots = lax.dynamic_slice_in_dim(child_slots, row_id * child_count, child_count)
    chosen = jnp.take(whole_front, row_slots, axis=0)
    residue_one = child_back[0] - sum_rows(matmul(child_low[0].T, spread_cols(chosen)))
    child_x = sum_cols(matmul(child_tile.T, spread_rows(residue_one.astype(jnp.bfloat16))))
    return (child_up[None], parent_up[None], root_up[None], child_x[None], parent_x[None], root_x)


def solution(mesh):
    return jax.shard_map(
        per_device,
        mesh=mesh,
        in_specs=(
            P("sec", "col", "row"),
            P("sec", "row", "col"),
            P("sec", "col", "row"),
            P("sec", "row", "col"),
            P("col", ("sec", "row")),
            P(),
            P(),
            P("sec", "row", "col"),
            P("sec", "row", "col"),
            P(("sec", "row"), "col"),
            P("sec", "col", "row"),
            P("sec", "col", "row"),
            P("col", ("sec", "row"), None),
        ),
        out_specs=(
            P("sec", "col", "row"),
            P("sec", "col", "row"),
            P("col", ("sec", "row"), None),
            P("sec", "row", "col"),
            P("sec", "row", "col"),
            P(("sec", "row"), "col"),
        ),
        check_vma=False,
    )
```

profile of v0, /device:TPU:1, one launch (start us, length us, event | category | flops | bytes accessed | tf_op | source)
XLA Modules:
  0.0 645.2 jit_solution(9738910207245959300)
XLA Ops:
  8.1 1.7 convert_element_type.59
  9.9 50.4 %all-gather.16.cloned.1.call-done = bf16[1,3072,512]{2,1,0:T(8,128)(2,1)} async-done(((bf16[1,96,512]{2,1,0:T(8,128)(2,1)}), bf16[1,3072,512]{2,1,0:T(8,128)(2,1)}) %all-gather.16.cloned.1.call-update) | async-done | bytes 3145744 | tf_op jit(solution)/shard_map/all_gather | solution.py:41
  60.3 4.2 fusion.1
  64.5 20.7 %reduce-scatter.27.cloned.1.call-done = f32[384,128]{1,0:T(8,128)} async-done(((f32[384,512]{1,0:T(8,128)}), f32[384,128]{1,0:T(8,128)}) %reduce-scatter.27.cloned.1.call-update) | async-done | bytes 196624 | tf_op jit(solution)/shard_map/reduce_scatter | solution.py:29
  86.9 11.6 %all-gather = bf16[1,512,512]{2,1,0:T(8,128)(2,1)S(1)} all-gather(bf16[1,512,128]{2,1,0:T(8,128)(2,1)S(1)} %convert_element_type.49), channel_id=2, replica_groups=mesh['sec'=4,'row'=8,'col'=4] {'col'}, dimensions={2}, use_global_device_ids=true | all-gather | bytes 655360 | tf_op jit(solution)/shard_map/all_gather | solution.py:17
  98.5 3.4 fusion.18
  102.8 32.5 %all-gather.10.cloned.1.call-done = bf16[12288,128]{1,0:T(8,128)(2,1)} async-done(((bf16[384,128]{1,0:T(8,128)(2,1)}), bf16[12288,128]{1,0:T(8,128)(2,1)}) %all-gather.10.cloned.1.call-update) | async-done | bytes 3145744 | tf_op jit(solution)/shard_map/all_gather | solution.py:41
  135.3 3.0 gather_fusion
  138.4 10.5 %all_gather.43 = bf16[256,512]{0,1:T(8,128)(2,1)S(1)} all-gather(bf16[256,128]{0,1:T(8,128)(2,1)S(1)} %broadcast_select_fusion), channel_id=1, replica_groups=mesh['sec'=4,'row'=8,'col'=4] {'col'}, dimensions={1}, use_global_device_ids=true | all-gather | bytes 327680 | tf_op jit(solution)/shard_map/all_gather | solution.py:17
  150.6 1.6 convert_element_type.51
  152.3 28.8 %reduce-scatter.29.cloned.1.call-done = f32[768,64]{0,1:T(8,128)} async-done(((f32[768,512]{0,1:T(8,128)}), f32[768,64]{0,1:T(8,128)}) %reduce-scatter.29.cloned.1.call-update) | async-done | bytes 196624 | tf_op jit(solution)/shard_map/reduce_scatter | solution.py:25
  182.2 17.9 %all_gather.44 = bf16[768,512]{0,1:T(8,128)(2,1)} all-gather(bf16[768,64]{0,1:T(8,128)(2,1)S(1)} %fusion.27), channel_id=1, replica_groups=mesh['sec'=4,'row'=8,'col'=4] {'row'}, dimensions={1}, use_global_device_ids=true | all-gather | bytes 884736 | tf_op jit(solution)/shard_map/all_gather | solution.py:21
  201.3 7.4 %all-gather.8.cloned.1.call-done = bf16[1024,512]{0,1:T(8,128)(2,1)} async-done(((bf16[1024,64]{0,1:T(8,128)(2,1)}), bf16[1024,512]{0,1:T(8,128)(2,1)}) %all-gather.8.cloned.1.call-update) | async-done | bytes 1048592 | tf_op jit(solution)/shard_map/all_gather | solution.py:21
  208.7 2.5 convolution_bitcast_fusion.5
  211.3 8.1 %collective-permute-done.3 = bf16[768,512]{0,1:T(8,128)(2,1)} collective-permute-done((bf16[768,512]{0,1:T(8,128)(2,1)}, bf16[768,512]{0,1:T(8,128)(2,1)}, u32[]{:S(2)}, u32[]{:S(2)}) %collective-permute-start.3) | collective-permute-done | bytes 786464 | tf_op jit(solution)/shard_map/ppermute | solution.py:13
  219.4 4.3 fusion.14
  224.0 7.1 %reduce-scatter.17.cloned.1.call-done = f32[256,128]{0,1:T(8,128)} async-done(((f32[256,512]{0,1:T(8,128)}), f32[256,128]{0,1:T(8,128)}) %reduce-scatter.17.cloned.1.call-update) | async-done | bytes 131088 | tf_op jit(solution)/shard_map/reduce_scatter | solution.py:29
  232.8 4.0 scatter_custom_fusion
  236.8 5.6 copy.40
  242.5 13.7 %reduce-scatter.31.cloned.1.call-done = f32[384,128]{0,1:T(8,128)} async-done(((f32[384,512]{0,1:T(8,128)}), f32[384,128]{0,1:T(8,128)}) %reduce-scatter.31.cloned.1.call-update) | async-done | bytes 196624 | tf_op jit(solution)/shard_map/reduce_scatter | solution.py:29
  257.9 38.9 %reduce-scatter.19.cloned.1.call-done = f32[2,512,128]{1,2,0:T(8,128)} async-done(((f32[2,4096,128]{1,2,0:T(8,128)}), f32[2,512,128]{1,2,0:T(8,128)}) %reduce-scatter.19.cloned.1.call-update) | async-done | bytes 524304 | tf_op jit(solution)/shard_map/reduce_scatter | solution.py:112
  299.1 1.7 copy.38
  300.8 2.4 collective-permute-done
  305.2 10.8 %all_gather.38 = bf16[384,512]{0,1:T(8,128)(2,1)S(1)} all-gather(bf16[384,128]{0,1:T(8,128)(2,1)S(1)} %fusion.26), channel_id=1, replica_groups=mesh['sec'=4,'row'=8,'col'=4] {'col'}, dimensions={1}, use_global_device_ids=true | all-gather | bytes 491520 | tf_op jit(solution)/shard_map/all_gather | solution.py:17
  316.0 3.9 convolution_bitcast_fusion
  321.4 16.7 %collective-permute-done.4 = bf16[4096,128]{0,1:T(8,128)(2,1)S(1)} collective-permute-done((bf16[4096,128]{0,1:T(8,128)(2,1)}, bf16[4096,128]{0,1:T(8,128)(2,1)S(1)}, u32[]{:S(2)}, u32[]{:S(2)}) %collective-permute-start.4) | collective-permute-done | bytes 1048608 | tf_op jit(solution)/shard_map/ppermute | solution.py:13
  338.1 3.5 maximum_select_fusion
  341.6 4.1 copy.43
  345.7 3.2 gather_fusion.1
  351.3 9.5 %all_gather.46 = bf16[256,512]{0,1:T(8,128)(2,1)S(1)} all-gather(bf16[256,128]{0,1:T(8,128)(2,1)S(1)} %broadcast_select_fusion.1), channel_id=1, replica_groups=mesh['sec'=4,'row'=8,'col'=4] {'col'}, dimensions={1}, use_global_device_ids=true | all-gather | bytes 327680 | tf_op jit(solution)/shard_map/all_gather | solution.py:17
  360.9 1.8 convolution_bitcast_fusion.1
  365.0 3.6 collective-permute-done.1
  368.6 1.7 fusion.28
  370.3 29.6 %all_gather.39 = bf16[768,512]{0,1:T(8,128)(2,1)S(1)} all-gather(bf16[768,64]{0,1:T(8,128)(2,1)S(1)} %get-tuple-element.30), channel_id=1, replica_groups=mesh['sec'=4,'row'=8,'col'=4] {'row'}, dimensions={1}, use_global_device_ids=true | all-gather | bytes 884736 | tf_op jit(solution)/shard_map/all_gather | solution.py:21
  401.3 7.6 %reduce-scatter.33.cloned.1.call-done = f32[1024,64]{0,1:T(8,128)} async-done(((f32[1024,512]{0,1:T(8,128)}), f32[1024,64]{0,1:T(8,128)}) %reduce-scatter.33.cloned.1.call-update) | async-done | bytes 262160 | tf_op jit(solution)/shard_map/reduce_scatter | solution.py:25
  408.8 1.6 fusion.25
  410.5 22.1 %reduce-scatter.23.cloned.1.call-done = f32[256,128]{0,1:T(8,128)} async-done(((f32[256,512]{0,1:T(8,128)}), f32[256,128]{0,1:T(8,128)}) %reduce-scatter.23.cloned.1.call-update) | async-done | bytes 131088 | tf_op jit(solution)/shard_map/reduce_scatter | solution.py:29
  437.6 4.0 scatter_custom_fusion.1
  441.6 4.2 convert_element_type.54
  445.9 14.0 %all-gather.14.cloned.1.call-done = bf16[1024,512]{0,1:T(8,128)(2,1)} async-done(((bf16[1024,64]{0,1:T(8,128)(2,1)}), bf16[1024,512]{0,1:T(8,128)(2,1)}) %all-gather.14.cloned.1.call-update) | async-done | bytes 1048592 | tf_op jit(solution)/shard_map/all_gather | solution.py:21
  459.9 3.0 convolution_bitcast_fusion.3
  462.9 64.2 %reduce-scatter.25.cloned.1.call-done = bf16[384,128]{1,0:T(8,128)(2,1)} async-done(((bf16[12288,128]{1,0:T(8,128)(2,1)}), bf16[384,128]{1,0:T(8,128)(2,1)}) %reduce-scatter.25.cloned.1.call-update) | async-done | bytes 98320 | tf_op jit(solution)/shard_map/reduce_scatter | solution.py:130
  528.1 10.1 %all_gather.40 = bf16[384,512]{1,0:T(8,128)(2,1)S(1)} all-gather(bf16[384,128]{1,0:T(8,128)(2,1)S(1)} %add_convert_fusion), channel_id=1, replica_groups=mesh['sec'=4,'row'=8,'col'=4] {'col'}, dimensions={1}, use_global_device_ids=true | all-gather | bytes 491520 | tf_op jit(solution)/shard_map/all_gather | solution.py:17
  538.2 3.5 fusion
  541.8 4.7 copy.48
  548.2 5.8 reduce-scatter.35.cloned.1.call-done
  554.0 1.8 copy.46
  555.7 80.5 %reduce-scatter.37.cloned.1.call-done = bf16[96,512]{1,0:T(8,128)(2,1)} async-done(((bf16[3072,512]{1,0:T(8,128)(2,1)}), bf16[96,512]{1,0:T(8,128)(2,1)}) %reduce-scatter.37.cloned.1.call-update) | async-done | bytes 98320
  (96 shorter events, 31.9 us)
Async XLA Ops:
  8.0 52.3 %copy-start = (bf16[3072,384]{1,0:T(8,128)(2,1)S(1)}, bf16[3072,384]{1,0:T(8,128)(2,1)}, u32[]{:S(2)}) copy-start(bf16[3072,384]{1,0:T(8,128)(2,1)} %param.17) | copy-start | bytes 7077892
  8.0 52.3 %all-gather.16.cloned.1.call-start = ((), (), s32[]{:S(2)}) async-start(), calls=%async_computation.27 | async-start | bytes 3244032 | tf_op jit(solution)/shard_map/all_gather | solution.py:41
  9.8 77.1 %copy-start.5 = (f32[1,512,128]{2,1,0:T(8,128)S(1)}, f32[1,512,128]{2,1,0:T(8,128)}, u32[]{:S(2)}) copy-start(f32[1,512,128]{2,1,0:T(8,128)} %param.20) | copy-start | bytes 786436
  9.8 75.4 %reduce-scatter.27.cloned.1.call-start = ((), (), s32[]{:S(2)}) async-start(), calls=%async_computation.19 | async-start | bytes 983040 | tf_op jit(solution)/shard_map/reduce_scatter | solution.py:29
  64.5 70.8 %all-gather.10.cloned.1.call-start = ((), (), s32[]{:S(2)}) async-start(), calls=%async_computation.20 | async-start | bytes 3244032 | tf_op jit(solution)/shard_map/all_gather | solution.py:41
  86.8 63.8 %reduce-scatter.15.cloned.1.call-start = ((), (), s32[]{:S(2)}) async-start(), calls=%async_computation.12 | async-start | bytes 2359296 | tf_op jit(solution)/shard_map/reduce_scatter | solution.py:25
  98.5 50.5 %copy-start.2 = (bf16[1,256,768]{2,1,0:T(8,128)(2,1)S(1)}, bf16[1,256,768]{2,1,0:T(8,128)(2,1)}, u32[]{:S(2)}) copy-start(bf16[1,256,768]{2,1,0:T(8,128)(2,1)} %param.16) | copy-start | bytes 1179652
  101.9 79.2 %reduce-scatter.29.cloned.1.call-start = ((), (), s32[]{:S(2)}) async-start(), calls=%async_computation.21 | async-start | bytes 1769472 | tf_op jit(solution)/shard_map/reduce_scatter | solution.py:25
  138.3 70.4 %copy-start.1 = (bf16[1,256,1024]{2,1,0:T(8,128)(2,1)S(1)}, bf16[1,256,1024]{2,1,0:T(8,128)(2,1)}, u32[]{:S(2)}) copy-start(bf16[1,256,1024]{2,1,0:T(8,128)(2,1)} %param.14) | copy-start | bytes 1572868
  150.5 58.1 %all-gather.8.cloned.1.call-start = ((), (), s32[]{:S(2)}) async-start(), calls=%async_computation.13 | async-start | bytes 1179648 | tf_op jit(solution)/shard_map/all_gather | solution.py:21
  152.3 78.9 %reduce-scatter.17.cloned.1.call-start = ((), (), s32[]{:S(2)}) async-start(), calls=%async_computation.14 | async-start | bytes 655360 | tf_op jit(solution)/shard_map/reduce_scatter | solution.py:29
  200.1 19.3 %collective-permute-start.3 = (bf16[768,512]{0,1:T(8,128)(2,1)}, bf16[768,512]{0,1:T(8,128)(2,1)}, u32[]{:S(2)}, u32[]{:S(2)}) collective-permute-start(bf16[768,512]{0,1:T(8,128)(2,1)} %all_gather.44), channel_id=1, source_target_pairs={{0,32},{32,0},{64,96},{96,64},{1,33},{33,1},{65,97},{97,65},{2,34}... | collective-permute-start | bytes 2359304 | tf_op jit(solution)/shard_map/ppermute | solution.py:13
  211.2 45.0 %reduce-scatter.31.cloned.1.call-start = ((), (), s32[]{:S(2)}) async-start(), calls=%async_computation.22 | async-start | bytes 983040 | tf_op jit(solution)/shard_map/reduce_scatter | solution.py:29
  211.2 12.5 %copy-start.7 = (s32[4,2048]{1,0:T(4,128)S(1)}, s32[4,2048]{1,0:T(4,128)}, u32[]{:S(2)}) copy-start(s32[4,2048]{1,0:T(4,128)} %param.18) | copy-start | bytes 98308
  223.7 73.1 %reduce-scatter.19.cloned.1.call-start = ((), (), s32[]{:S(2)}) async-start(), calls=%async_computation.15 | async-start | bytes 4718592 | tf_op jit(solution)/shard_map/reduce_scatter | solution.py:112
  242.4 77.6 %all-gather.12.cloned.1.call-start = ((), (), s32[]{:S(2)}) async-start(), calls=%async_computation.23 | async-start | bytes 1179648 | tf_op jit(solution)/shard_map/all_gather | solution.py:150
  257.9 104.9 %reduce-scatter.21.cloned.1.call-start = ((), (), s32[]{:S(2)}) async-start(), calls=%async_computation.16 | async-start | bytes 3538944 | tf_op jit(solution)/shard_map/reduce_scatter | solution.py:25
  297.8 5.4 collective-permute-start
  320.0 88.9 %reduce-scatter.33.cloned.1.call-start = ((), (), s32[]{:S(2)}) async-start(), calls=%async_computation.24 | async-start | bytes 2359296 | tf_op jit(solution)/shard_map/reduce_scatter | solution.py:25
  320.0 18.1 %collective-permute-start.4 = (bf16[4096,128]{0,1:T(8,128)(2,1)}, bf16[4096,128]{0,1:T(8,128)(2,1)S(1)}, u32[]{:S(2)}, u32[]{:S(2)}) collective-permute-start(bf16[4096,128]{0,1:T(8,128)(2,1)} %all-gather.12.cloned.1.call-done), channel_id=1, source_target_pairs={{0,32},{32,0},{64,96},{96,64},{1,33},{33,1},{65,97},{97,65},{2,34}... | collective-permute-start | bytes 3145736 | tf_op jit(solution)/shard_map/ppermute | solution.py:13
  362.6 46.2 %copy-start.6 = (f32[1,1024,64]{1,2,0:T(8,128)S(1)}, f32[1,1024,64]{1,2,0:T(8,128)}, u32[]{:S(2)}) copy-start(f32[1,1024,64]{1,2,0:T(8,128)} %param.23) | copy-start | bytes 786436
  362.7 70.0 %reduce-scatter.23.cloned.1.call-start = ((), (), s32[]{:S(2)}) async-start(), calls=%async_computation.17 | async-start | bytes 655360 | tf_op jit(solution)/shard_map/reduce_scatter | solution.py:29
  363.7 4.9 collective-permute-start.1
  401.2 58.7 %all-gather.14.cloned.1.call-start = ((), (), s32[]{:S(2)}) async-start(), calls=%async_computation.25 | async-start | bytes 1179648 | tf_op jit(solution)/shard_map/all_gather | solution.py:21
  410.5 116.6 %reduce-scatter.25.cloned.1.call-start = ((), (), s32[]{:S(2)}) async-start(), calls=%async_computation.18 | async-start | bytes 3244032 | tf_op jit(solution)/shard_map/reduce_scatter | solution.py:130
  433.5 3.1 collective-permute-start.2
  445.8 14.1 %copy-start.3 = (bf16[1,1024,512]{2,1,0:T(8,128)(2,1)S(1)}, bf16[1,1024,512]{2,1,0:T(8,128)(2,1)}, u32[]{:S(2)}) copy-start(bf16[1,1024,512]{2,1,0:T(8,128)(2,1)} %param.13) | copy-start | bytes 3145732
  445.8 108.1 %reduce-scatter.35.cloned.1.call-start = ((), (), s32[]{:S(2)}) async-start(), calls=%async_computation.26 | async-start | bytes 1310720 | tf_op jit(solution)/shard_map/reduce_scatter | solution.py:29
  462.9 173.4 %reduce-scatter.37.cloned.1.call-start = ((), (), s32[]{:S(2)}) async-start(), calls=%async_computation.28 | async-start | bytes 3244032
  546.4 0.9 copy-start.4
Sparse Core Ops, SparseCore 0:
  11.7 48.5 all-gather.15
  64.6 20.5 reduce-scatter.26
  88.1 47.1 all-gather.9
  211.3 19.7 reduce-scatter.16
  233.4 22.8 reduce-scatter.30
  258.5 38.2 reduce-scatter.18
  446.0 81.0 reduce-scatter.24
  529.6 24.2 reduce-scatter.34
  557.6 78.6 reduce-scatter.36
Sparse Core Ops, SparseCore 1:
  102.0 37.3 reduce-scatter.14
  150.6 30.5 reduce-scatter.28
  183.3 25.3 all-gather.7
  257.9 28.7 all-gather.11
  320.0 37.7 reduce-scatter.20
  362.8 46.0 reduce-scatter.32
  411.1 21.5 reduce-scatter.22
  434.9 24.9 all-gather.13
where the time goes:
time: 647 us; the launch traced here: 645 us
  waiting for transfers between devices  426 us (66%)
  blocking collectives  100 us (15%)
  other arithmetic  34.2 us (5%)
  local copies, waits for them, and re-layouts  33 us (5%)
  matrix products  29.3 us (5%)
  between operations  15.7 us (2%)
  starting transfers between devices  6.62 us (1%)
    all_gather x2, waiting for transfers between devices, root_gather(): return lax.all_gather(block, ('sec', 'row'), axis=0, tiled=True)  82.9 us
    unnamed x18, waiting for transfers between devices  80.8 us
    reduce_scatter x5, waiting for transfers between devices, sum_cols(): return lax.psum_scatter(block, 'col', scatter_dimension=1, tiled=True)  69.4 us
    reduce_scatter x1, waiting for transfers between devices, per_device(): lax.psum_scatter(dense_root.astype(jnp.bfloat16), ('sec', 'row'), scatter...  64.2 us
    all_gather x5, blocking collectives, spread_cols(): return lax.all_gather(block, 'col', axis=1, tiled=True)  52.6 us
    all_gather x2, blocking collectives, spread_rows(): return lax.all_gather(block, 'row', axis=1, tiled=True)  47.5 us
    reduce_scatter x1, waiting for transfers between devices, per_device(): lax.psum_scatter(dense.reshape(2, n_row * stride, contrib.shape[1]), 'row...  38.9 us
    reduce_scatter x4, waiting for transfers between devices, sum_rows(): return lax.psum_scatter(block, 'row', scatter_dimension=1, tiled=True)  36.4 us
  transfers between devices with their start and end apart: 22, of which 19 were waited for; matrix products, arithmetic and copies ran while one was open for 13% of the time, Pallas kernels for 0%

commit v1 on v0

v1 whole, which is shorter than its diff:
```python
import types

import jax
import jax.numpy as jnp
from jax import lax
from jax.experimental import pallas as pl
from jax.experimental.pallas import tpu as pltpu
from jax.sharding import PartitionSpec as P

BF = jnp.bfloat16
F32 = jnp.float32
I32 = jnp.int32
MESH = pl.DeviceIdType.MESH

INPUTS = dict(
    wci=((1024, 512), BF),
    wcl=((256, 1024), BF),
    wpi=((1536, 384), BF),
    wpl=((256, 768), BF),
    wr=((3072, 384), BF),
    cmap=((4, 2048), I32),
    pmap=((2, 2048), I32),
    i_cr=((512, 128), F32),
    i_pr=((384, 128), F32),
    i_rr=((384, 128), F32),
    i_cb=((64, 1024), F32),
    i_pb=((64, 768), F32),
    i_rb=((96, 512), F32),
)
OUTPUTS = dict(
    o_cu=((64, 1024), F32),
    o_pu=((64, 768), F32),
    o_ru=((96, 512), F32),
    o_cx=((512, 128), F32),
    o_px=((384, 128), F32),
    o_rx=((384, 128), F32),
)
SCRATCH = dict(
    sel=((512, 4096), BF),
    rsel=((384, 4096), BF),
    f_x=((4, 512, 128), BF),
    f_ps=((4, 512, 128), BF),
    f_pr=((4, 512, 128), BF),
    f_xs=((3, 512, 128), BF),
    f_xr=((3, 512, 128), BF),
    f_u=((512, 128), F32),
    f_us=((512, 128), F32),
    f_x2=((4, 2, 512, 128), BF),
    f_cs=((3, 256, 128), BF),
    f_cr=((3, 256, 128), BF),
    f_c=((2, 8, 256, 128), BF),
    f_fc=((128, 128), F32),
    f_px=((4, 384, 128), BF),
    f_qs=((4, 768, 128), BF),
    f_k=((4, 768, 128), F32),
    f_qr=((4, 768, 128), BF),
    f_qxs=((3, 768, 128), BF),
    f_qxr=((3, 768, 128), BF),
    f_q=((768, 128), F32),
    f_qps=((384, 128), BF),
    f_qpr=((384, 128), BF),
    f_pu=((384, 128), F32),
    f_pus=((384, 128), F32),
    f_x3=((4, 2, 384, 128), BF),
    f_ds=((3, 256, 128), BF),
    f_dr=((3, 256, 128), BF),
    f_up=((2, 128, 128), F32),
    f_ups=((128, 128), BF),
    f_upr=((128, 128), BF),
    f_r=((2, 8, 2, 128, 128), BF),
    f_rx=((4, 384, 128), BF),
    f_t=((2, 4, 4, 96, 512), BF),
    f_tr=((4, 4, 96, 512), BF),
    f_as=((3, 4, 96, 256), BF),
    f_bs=((3, 4, 96, 256), BF),
    f_ar=((3, 4, 96, 256), BF),
    f_br=((3, 4, 96, 256), BF),
    f_oa=((4, 96, 256), F32),
    f_ob=((4, 96, 256), F32),
    f_a2s=((3, 96, 256), BF),
    f_b2s=((3, 96, 256), BF),
    f_a2r=((3, 96, 256), BF),
    f_b2r=((3, 96, 256), BF),
    b_y=((4, 4, 2, 96, 512), BF),
    b_r=((4, 384, 128), F32),
    b_rs=((3, 384, 128), BF),
    b_rr=((3, 384, 128), BF),
    b_rx=((384, 128), BF),
    b_t=((2, 4, 2, 256, 128), BF),
    b_tr=((2, 4, 256, 128), BF),
    b_txs=((3, 2, 256, 128), BF),
    b_txr=((3, 2, 256, 128), BF),
    b_tp=((2, 256, 128), BF),
    b_tpr=((3, 256, 128), BF),
    b_pk=((4, 256, 128), BF),
    b_es=((4, 384, 128), BF),
    b_er=((4, 384, 128), BF),
    b_exs=((3, 384, 128), BF),
    b_exr=((3, 384, 128), BF),
    b_pbs=((64, 768), F32),
    b_g=((4, 2, 2, 384, 128), BF),
    b_hs=((3, 384, 128), BF),
    b_hr=((3, 384, 128), BF),
    b_fx=((512, 128), BF),
    b_v=((2, 4, 2, 256, 128), BF),
    b_vr=((2, 4, 256, 128), BF),
    b_vxs=((3, 2, 256, 128), BF),
    b_vxr=((3, 2, 256, 128), BF),
    b_vp=((2, 256, 128), BF),
    b_vpr=((256, 128), BF),
    b_ck=((4, 256, 128), BF),
    b_ls=((4, 512, 128), BF),
    b_k=((4, 512, 128), F32),
    b_lr=((4, 512, 128), BF),
    b_lxs=((3, 512, 128), BF),
    b_lxr=((3, 512, 128), BF),
    b_cbs=((64, 1024), F32),
    b_h=((4, 2, 512, 128), BF),
    b_ms=((3, 512, 128), BF),
    b_mr=((3, 512, 128), BF),
)
N_REMOTE = 180
N_LOCAL = len(INPUTS) + len(OUTPUTS)


def dot(a, b):
    return jnp.dot(a, b, preferred_element_type=F32)


def dot_t(a, b):
    return lax.dot_general(a, b, (((0,), (0,)), ((), ())), preferred_element_type=F32)


def body(*refs):
    n_in, n_out = len(INPUTS), len(OUTPUTS)
    hbm_in = refs[:n_in]
    hbm_out = refs[n_in : n_in + n_out]
    rest = refs[n_in + n_out :]
    names = [*INPUTS, *OUTPUTS, *SCRATCH]
    v = types.SimpleNamespace(**dict(zip(names, rest)))
    send_sems, recv_sems, local_sems = rest[len(names) :]

    sec = lax.axis_index("sec")
    row = lax.axis_index("row")
    z = lax.axis_index("col")
    x = row // 2
    c = row % 2
    sib = 1 - c
    h = sec % 2
    p = sec // 2
    oh = 1 - h

    def at_x(d):
        return {"row": ((x + d) % 4) * 2 + c}

    def at_y(d):
        return {"sec": (sec + d) % 4}

    def at_z(d):
        return {"col": (z + d) % 4}

    sibling = {"row": x * 2 + sib}
    pair = {"sec": p * 2 + oh}

    loads = {}
    for i, (ref, src) in enumerate(zip(rest, hbm_in)):
        if len(src.shape) > len(ref.shape):
            src = src.at[0]
        loads[id(ref)] = pltpu.make_async_copy(src, ref, local_sems.at[i])
    first = (v.i_rb, v.i_cr, v.i_cb, v.i_pb, v.wci, v.wr, v.cmap, v.pmap)
    for ref in first + (v.wcl, v.i_pr, v.wpi, v.wpl, v.i_rr):
        loads[id(ref)].start()

    def need(*wanted):
        for ref in wanted:
            copy = loads.pop(id(ref), None)
            if copy is not None:
                copy.wait()

    stores = []

    def emit(ref, i):
        dst = hbm_out[i]
        if len(dst.shape) > 2:
            dst = dst.at[0]
        copy = pltpu.make_async_copy(ref, dst, local_sems.at[n_in + i])
        copy.start()
        stores.append(copy)

    barrier = pltpu.get_barrier_semaphore()
    peers = [sibling] + [f(d) for f in (at_x, at_y, at_z) for d in (1, 2, 3)]
    for peer in peers:
        pl.semaphore_signal(barrier, inc=1, device_id=peer, device_id_type=MESH)
    pl.semaphore_wait(barrier, len(peers))

    sent = []

    def send(src, dst, peer):
        n = len(sent)
        copy = pltpu.make_async_remote_copy(
            src_ref=src,
            dst_ref=dst,
            send_sem=send_sems.at[n],
            recv_sem=recv_sems.at[n],
            device_id=peer,
            device_id_type=MESH,
        )
        copy.start()
        sent.append(copy)
        return copy

    def arrive(copies):
        for copy in copies:
            copy.wait_recv()

    def spread(ref, where):
        return [send(ref, ref, where(d)) for d in (1, 3, 2)]

    def lanes(full):
        turned = full.T
        return jnp.where(c == 0, turned[:64], turned[64:])

    def both(mine, other):
        first = jnp.where(c == 0, mine, other)
        second = jnp.where(c == 0, other, mine)
        return jnp.concatenate([first, second], axis=0).T

    def tiles(count, size):
        def wrap(step):
            @pl.loop(0, count // size)
            def _(i):
                step(pl.ds(pl.multiple_of(i * size, size), size))

        return wrap

    def build(ref, base_of, table, first):
        count = ref.shape[0]

        @pl.loop(0, 16)
        def _(k):
            at = pl.multiple_of(lax.rem(k, 8) * 256, 256)
            part = table[pl.ds(first + k // 8, 1), pl.ds(at, 256)]
            for lo in range(0, count, 128):
                target = base_of(lax.broadcasted_iota(I32, (128, 256), 0) + lo)
                hit = jnp.where(jnp.broadcast_to(part, (128, 256)) == target, 1.0, 0.0)
                ref[lo : lo + 128, pl.ds(pl.multiple_of(k * 256, 256), 256)] = hit.astype(BF)

    def wide(src, depth):
        parts = [src[j].reshape(depth, 128) for j in range(4)]
        return jnp.concatenate(parts, axis=1)

    def back_mm(w, start, src, depth, out):
        @tiles(out.shape[1], 128)
        def _(m):
            at = pl.ds(pl.multiple_of(start + m.start, 128), 128)
            r = dot_t(w[:, at], wide(src, depth))
            for j in range(4):
                out[j, m, :] = r[:, j * 128 : (j + 1) * 128].astype(out.dtype)

    def pick(matrix, vec, out):
        @pl.loop(0, 8)
        def _(k):
            r = dot_t(matrix[:, pl.ds(pl.multiple_of(k * 512, 512), 512)], vec[...])
            out[k // 4, lax.rem(k, 4)] = r.astype(BF).reshape(2, 256, 128)

    def hand_on(keep, part, buf, count):
        @tiles(count, 128)
        def _(m):
            buf[m, :] = (keep[m, :] + part[m, :].astype(F32)).astype(BF)

    def tot(part, m):
        return (part[0, m, :].astype(F32) + part[1, m, :].astype(F32)) + part[2, m, :].astype(F32)

    def root_sum(s, k, lo):
        mine = v.f_t[c, s, k, :, lo : lo + 256].astype(F32)
        return mine + v.f_tr[s, k, :, lo : lo + 256].astype(F32)

    def child_base(j):
        return jnp.where(
            j < 384, h * 3072 + row * 384 + j, 6144 - 384 + row * 256 + h * 128 + j
        )

    def root_base(j):
        return (sec * 8 + row) * 384 + j

    def forward():
        need(v.i_cr)
        v.f_x[z] = v.i_cr[...].astype(BF)
        got = spread(v.f_x.at[z], at_z)
        yield
        need(v.cmap)
        build(v.sel, child_base, v.cmap, 2 * p)
        need(v.wci)
        core = []
        order = (0, 1, 3, 2)
        for d in order:
            if d:
                got[order.index(d) - 1].wait_recv()
            ch = (z + 4 - d) % 4
            v.f_ps[ch] = dot(v.wci[pl.ds(sib * 512, 512), :], v.f_x[ch]).astype(BF)
            core.append(send(v.f_ps.at[ch], v.f_pr.at[ch], sibling))
        for ch in range(4):
            v.f_k[ch, :512] = dot(v.wci[pl.ds(c * 512, 512), :], v.f_x[ch])
        yield
        arrive(core)
        got = []
        for d in (1, 3, 2):
            ch = (x + d) % 4
            hand_on(v.f_k.at[ch], v.f_pr.at[ch], v.f_xs.at[d - 1], 512)
            got.append(send(v.f_xs.at[d - 1], v.f_xr.at[d - 1], at_x(d)))
        yield
        arrive(got)

        @tiles(512, 128)
        def _(m):
            own = (v.f_k[x, m, :] + v.f_pr[x, m, :].astype(F32)) + tot(v.f_xr, m)
            v.f_x2[x, c, m, :] = own.astype(BF)
            v.f_u[m, :] = own

        got = spread(v.f_x2.at[x, c], at_x)
        core = [send(v.f_x2.at[x, c], v.f_x2.at[x, c], sibling)]
        up = send(v.f_u, v.f_us, sibling)
        yield
        need(v.wcl)
        for copy, d in zip(got, (1, 3, 2)):
            copy.wait_recv()
            ref = v.f_x2.at[(x + 4 - d) % 4, c]
            core.append(send(ref, ref, sibling))
        yield
        arrive(core)
        got = []
        for d in (1, 3, 2):
            ch = (z + d) % 4
            r = dot(v.wcl[...], v.f_x2[ch].reshape(1024, 128))
            v.f_cs[d - 1] = r.astype(BF)
            got.append(send(v.f_cs.at[d - 1], v.f_cr.at[d - 1], at_z(d)))
        own = dot(v.wcl[...], v.f_x2[z].reshape(1024, 128))
        yield
        arrive(got)
        own = own + (v.f_cr[0].astype(F32) + v.f_cr[1].astype(F32)) + v.f_cr[2].astype(F32)
        v.f_c[h, row] = (-own).astype(BF)
        got = send(v.f_c.at[h, row], v.f_c.at[h, row], pair)
        up.wait_recv()
        v.o_cu[:, pl.ds(pl.multiple_of(c * 512, 128), 512)] = lanes(v.f_u[...])
        v.o_cu[:, pl.ds(pl.multiple_of(sib * 512, 128), 512)] = lanes(v.f_us[...])
        emit(v.o_cu, 0)
        yield
        got.wait_recv()
        got = spread(v.f_c.at[:, row], at_x)
        core = [send(v.f_c.at[:, row], v.f_c.at[:, row], sibling)]
        yield
        need(v.i_pr)
        for copy, d in zip(got, (1, 3, 2)):
            copy.wait_recv()
            ref = v.f_c.at[:, ((x + 4 - d) % 4) * 2 + c]
            core.append(send(ref, ref, sibling))
        yield
        arrive(core)

        @tiles(384, 128)
        def _(m):
            front = dot(v.sel[m, :], v.f_c[...].reshape(4096, 128))
            v.f_px[z, m, :] = (v.i_pr[m, :] + front).astype(BF)

        got = spread(v.f_px.at[z], at_z)
        v.f_fc[...] = dot(v.sel[384:, :], v.f_c[...].reshape(4096, 128))
        yield
        need(v.wpi)
        core = []
        for d in order:
            if d:
                got[order.index(d) - 1].wait_recv()
            ch = (z + 4 - d) % 4
            for half in range(2):
                w = v.wpi[pl.ds(half * 768 + sib * 384, 384), :]
                v.f_qs[ch, half * 384 : (half + 1) * 384] = dot(w, v.f_px[ch]).astype(BF)
            core.append(send(v.f_qs.at[ch], v.f_qr.at[ch], sibling))
        for ch in range(4):
            for half in range(2):
                w = v.wpi[pl.ds(half * 768 + c * 384, 384), :]
                v.f_k[ch, half * 384 : (half + 1) * 384] = dot(w, v.f_px[ch])
        yield
        arrive(core)
        got = []
        for d in (1, 3, 2):
            ch = (x + d) % 4
            hand_on(v.f_k.at[ch], v.f_qr.at[ch], v.f_qxs.at[d - 1], 768)
            got.append(send(v.f_qxs.at[d - 1], v.f_qxr.at[d - 1], at_x(d)))
        yield
        arrive(got)

        @tiles(768, 128)
        def _(m):
            own = v.f_k[x, m, :] + v.f_qr[x, m, :].astype(F32)
            v.f_q[m, :] = own + tot(v.f_qxr, m)

        v.f_qps[...] = v.f_q[pl.ds(oh * 384, 384), :].astype(BF)
        got = send(v.f_qps, v.f_qpr, pair)
        yield
        got.wait_recv()
        own = v.f_q[pl.ds(h * 384, 384), :] + v.f_qpr[...].astype(F32)
        v.f_x3[x, c] = own.astype(BF)
        got = spread(v.f_x3.at[x, c], at_x)
        core = [send(v.f_x3.at[x, c], v.f_x3.at[x, c], sibling)]
        v.f_pu[...] = own
        up = send(v.f_pu, v.f_pus, sibling)
        yield
        need(v.wpl)
        for copy, d in zip(got, (1, 3, 2)):
            copy.wait_recv()
            ref = v.f_x3.at[(x + 4 - d) % 4, c]
            core.append(send(ref, ref, sibling))
        yield
        arrive(core)
        got = []
        for d in (1, 3, 2):
            ch = (z + d) % 4
            r = dot(v.wpl[...], v.f_x3[ch].reshape(768, 128))
            v.f_ds[d - 1] = r.astype(BF)
            got.append(send(v.f_ds.at[d - 1], v.f_dr.at[d - 1], at_z(d)))
        own = dot(v.wpl[...], v.f_x3[z].reshape(768, 128))
        yield
        arrive(got)
        own = own + (v.f_dr[0].astype(F32) + v.f_dr[1].astype(F32)) + v.f_dr[2].astype(F32)
        v.f_up[...] = own.reshape(2, 128, 128)
        v.f_ups[...] = v.f_up[oh].astype(BF)
        got = send(v.f_ups, v.f_upr, pair)
        up.wait_recv()
        v.o_pu[:, pl.ds(pl.multiple_of(c * 384, 128), 384)] = lanes(v.f_pu[...])
        v.o_pu[:, pl.ds(pl.multiple_of(sib * 384, 128), 384)] = lanes(v.f_pus[...])
        emit(v.o_pu, 1)
        yield
        got.wait_recv()
        own = v.f_fc[...] - (v.f_up[h] + v.f_upr[...].astype(F32))
        v.f_r[p, row, h] = own.astype(BF)
        got = spread(v.f_r.at[p, row, h], at_y)
        yield
        arrive(got)
        got = spread(v.f_r.at[:, row], at_x)
        core = [send(v.f_r.at[:, row], v.f_r.at[:, row], sibling)]
        yield
        need(v.i_rr)
        for copy, d in zip(got, (1, 3, 2)):
            copy.wait_recv()
            ref = v.f_r.at[:, ((x + 4 - d) % 4) * 2 + c]
            core.append(send(ref, ref, sibling))
        yield
        arrive(core)

        @tiles(384, 128)
        def _(m):
            front = dot(v.rsel[m, :], v.f_r[...].reshape(4096, 128))
            v.f_rx[z, m, :] = (v.i_rr[m, :] + front).astype(BF)

        got = spread(v.f_rx.at[z], at_z)
        yield
        arrive(got)
        core = []
        for s in range(4):

            @pl.loop(0, 4)
            def _(k):
                start = pl.multiple_of((s * 4 + k) * 192, 192)
                r = dot(v.wr[pl.ds(start, 192), :], wide(v.f_rx, 384))
                v.f_t[0, s, k] = r[:96].astype(BF)
                v.f_t[1, s, k] = r[96:].astype(BF)

            core.append(send(v.f_t.at[sib, s], v.f_tr.at[s], sibling))
        yield
        arrive(core)
        got_a, got_b = [], []
        for d in (1, 3, 2):
            ch = (x + d) % 4

            @pl.loop(0, 4)
            def _(s):
                v.f_as[d - 1, s] = root_sum(s, ch, 0).astype(BF)

            got_a.append(send(v.f_as.at[d - 1], v.f_ar.at[d - 1], at_x(d)))
            cy = (sec + d) % 4

            @pl.loop(0, 4)
            def _(s):
                v.f_bs[d - 1, s] = root_sum(cy, s, 256).astype(BF)

            got_b.append(send(v.f_bs.at[d - 1], v.f_br.at[d - 1], at_y(d)))

        @pl.loop(0, 4)
        def _(s):
            v.f_oa[s] = root_sum(s, x, 0)
            v.f_ob[s] = root_sum(sec, s, 256)

        yield
        for got, total, part in ((got_a, v.f_oa, v.f_ar), (got_b, v.f_ob, v.f_br)):
            arrive(got)

            @pl.loop(0, 4)
            def _(s):
                total[s] = total[s] + (
                    (part[0, s].astype(F32) + part[1, s].astype(F32))
                    + part[2, s].astype(F32)
                )

        got = []
        for d in (1, 3, 2):
            v.f_a2s[d - 1] = v.f_oa[(sec + d) % 4].astype(BF)
            got.append(send(v.f_a2s.at[d - 1], v.f_a2r.at[d - 1], at_y(d)))
            v.f_b2s[d - 1] = v.f_ob[(x + d) % 4].astype(BF)
            got.append(send(v.f_b2s.at[d - 1], v.f_b2r.at[d - 1], at_x(d)))
        yield
        arrive(got)
        for total, me, part, lo in ((v.f_oa, sec, v.f_a2r, 0), (v.f_ob, x, v.f_b2r, 256)):
            v.o_ru[:, lo : lo + 256] = total[me] + (
                (part[0].astype(F32) + part[1].astype(F32)) + part[2].astype(F32)
            )
        emit(v.o_ru, 2)

    def backward():
        need(v.i_rb)
        v.b_y[sec, x, c] = v.i_rb[...].astype(BF)
        ref_a = v.b_y.at[sec, x, c, :, 0:256]
        ref_b = v.b_y.at[sec, x, c, :, 256:512]
        got_a = spread(ref_a, at_x)
        got_b = spread(ref_b, at_y)
        need(v.i_cb, v.i_pb)
        cbs = send(v.i_cb, v.b_cbs, sibling)
        pbs = send(v.i_pb, v.b_pbs, sibling)
        yield
        need(v.pmap)
        build(v.rsel, root_base, v.pmap, 0)
        arrive(got_a)
        got = spread(v.b_y.at[sec, :, c, :, 0:256], at_y)
        arrive(got_b)
        got += spread(v.b_y.at[:, x, c, :, 256:512], at_x)
        yield
        arrive(got)
        core = [send(v.b_y.at[s, :, c], v.b_y.at[s, :, c], sibling) for s in range(4)]
        need(v.wr)
        yield
        for s in range(4):
            core[s].wait_recv()

            @tiles(384, 128)
            def _(m):
                r = dot_t(v.wr[s * 768 : (s + 1) * 768, m], v.b_y[s].reshape(768, 512))
                for j in range(4):
                    part = r[:, j * 128 : (j + 1) * 128]
                    v.b_r[j, m, :] = part if s == 0 else v.b_r[j, m, :] + part

        got = []
        for d in (1, 3, 2):
            v.b_rs[d - 1] = v.b_r[(z + d) % 4].astype(BF)
            got.append(send(v.b_rs.at[d - 1], v.b_rr.at[d - 1], at_z(d)))
        yield
        arrive(got)

        @tiles(384, 128)
        def _(m):
            own = v.b_r[z, m, :] + tot(v.b_rr, m)
            v.o_rx[m, :] = own
            v.b_rx[m, :] = own.astype(BF)

        emit(v.o_rx, 5)
        pick(v.rsel, v.b_rx, v.b_t)
        core = send(v.b_t.at[:, :, sib], v.b_tr, sibling)
        yield
        core.wait_recv()
        got = []
        for d in (1, 3, 2):
            ch = (x + d) % 4
            for q in range(2):
                v.b_txs[d - 1, q] = v.b_t[q, ch, c] + v.b_tr[q, ch]
            got.append(send(v.b_txs.at[d - 1], v.b_txr.at[d - 1], at_x(d)))
        yield
        arrive(got)
        for q in range(2):
            own = v.b_t[q, x, c] + v.b_tr[q, x]
            v.b_tp[q] = own + ((v.b_txr[0, q] + v.b_txr[1, q]) + v.b_txr[2, q])
        got = []
        for d in (1, 3, 2):
            got.append(send(v.b_tp.at[((sec + d) % 4) // 2], v.b_tpr.at[d - 1], at_y(d)))
        yield
        arrive(got)
        v.b_pk[z] = v.b_tp[p] + ((v.b_tpr[0] + v.b_tpr[1]) + v.b_tpr[2])
        got = spread(v.b_pk.at[z], at_z)
        yield
        need(v.wpl)
        arrive(got)
        back_mm(v.wpl, sib * 384, v.b_pk, 256, v.b_es)
        core = [send(v.b_es, v.b_er, sibling)]
        back_mm(v.wpl, c * 384, v.b_pk, 256, v.b_k.at[:, :384])
        yield
        arrive(core)
        got = []
        for d in (1, 3, 2):
            ch = (x + d) % 4
            hand_on(v.b_k.at[ch], v.b_er.at[ch], v.b_exs.at[d - 1], 384)
            got.append(send(v.b_exs.at[d - 1], v.b_exr.at[d - 1], at_x(d)))
        yield
        pbs.wait_recv()
        arrive(got)

        @tiles(384, 128)
        def _(m):
            at = pl.ds(pl.multiple_of(c * 384 + m.start, 128), 128)
            own = v.b_k[x, m, :] + v.b_er[x, m, :].astype(F32)
            own = both(v.i_pb[:, at], v.b_pbs[:, at]) - (own + tot(v.b_exr, m))
            v.b_g[x, h, c, m, :] = own.astype(BF)

        got = send(v.b_g.at[x, h, c], v.b_g.at[x, h, c], pair)
        yield
        got.wait_recv()
        got = spread(v.b_g.at[x, :, c], at_x)
        core = [send(v.b_g.at[x, :, c], v.b_g.at[x, :, c], sibling)]
        yield
        need(v.wpi)
        for copy, d in zip(got, (1, 3, 2)):
            copy.wait_recv()
            ref = v.b_g.at[(x + 4 - d) % 4, :, c]
            core.append(send(ref, ref, sibling))
        yield
        arrive(core)
        back_mm(v.wpi, 0, v.b_g, 1536, v.b_r)
        got = []
        for d in (1, 3, 2):
            v.b_hs[d - 1] = v.b_r[(z + d) % 4].astype(BF)
            got.append(send(v.b_hs.at[d - 1], v.b_hr.at[d - 1], at_z(d)))
        yield
        arrive(got)

        @tiles(384, 128)
        def _(m):
            own = v.b_r[z, m, :] + tot(v.b_hr, m)
            v.o_px[m, :] = own
            v.b_fx[m, :] = own.astype(BF)

        emit(v.o_px, 4)
        v.b_fx[384:, :] = v.b_pk[z, pl.ds(h * 128, 128), :]
        pick(v.sel, v.b_fx, v.b_v)
        core = send(v.b_v.at[:, :, sib], v.b_vr, sibling)
        yield
        core.wait_recv()
        got = []
        for d in (1, 3, 2):
            ch = (x + d) % 4
            for q in range(2):
                v.b_vxs[d - 1, q] = v.b_v[q, ch, c] + v.b_vr[q, ch]
            got.append(send(v.b_vxs.at[d - 1], v.b_vxr.at[d - 1], at_x(d)))
        yield
        arrive(got)
        for q in range(2):
            own = v.b_v[q, x, c] + v.b_vr[q, x]
            v.b_vp[q] = own + ((v.b_vxr[0, q] + v.b_vxr[1, q]) + v.b_vxr[2, q])
        got = send(v.b_vp.at[oh], v.b_vpr, pair)
        yield
        got.wait_recv()
        v.b_ck[z] = v.b_vp[h] + v.b_vpr[...]
        got = spread(v.b_ck.at[z], at_z)
        yield
        need(v.wcl)
        arrive(got)
        back_mm(v.wcl, sib * 512, v.b_ck, 256, v.b_ls)
        core = [send(v.b_ls, v.b_lr, sibling)]
        back_mm(v.wcl, c * 512, v.b_ck, 256, v.b_k)
        yield
        arrive(core)
        got = []
        for d in (1, 3, 2):
            ch = (x + d) % 4
            hand_on(v.b_k.at[ch], v.b_lr.at[ch], v.b_lxs.at[d - 1], 512)
            got.append(send(v.b_lxs.at[d - 1], v.b_lxr.at[d - 1], at_x(d)))
        yield
        cbs.wait_recv()
        arrive(got)

        @tiles(512, 128)
        def _(m):
            at = pl.ds(pl.multiple_of(c * 512 + m.start, 128), 128)
            own = v.b_k[x, m, :] + v.b_lr[x, m, :].astype(F32)
            own = both(v.i_cb[:, at], v.b_cbs[:, at]) - (own + tot(v.b_lxr, m))
            v.b_h[x, c, m, :] = own.astype(BF)

        got = spread(v.b_h.at[x, c], at_x)
        core = [send(v.b_h.at[x, c], v.b_h.at[x, c], sibling)]
        yield
        need(v.wci)
        for copy, d in zip(got, (1, 3, 2)):
            copy.wait_recv()
            ref = v.b_h.at[(x + 4 - d) % 4, c]
            core.append(send(ref, ref, sibling))
        yield
        arrive(core)
        back_mm(v.wci, 0, v.b_h, 1024, v.b_k)
        got = []
        for d in (1, 3, 2):
            v.b_ms[d - 1] = v.b_k[(z + d) % 4].astype(BF)
            got.append(send(v.b_ms.at[d - 1], v.b_mr.at[d - 1], at_z(d)))
        yield
        arrive(got)

        @tiles(512, 128)
        def _(m):
            v.o_cx[m, :] = v.b_k[z, m, :] + tot(v.b_mr, m)

        emit(v.o_cx, 3)

    chains = [backward(), forward()]
    while chains:
        for chain in list(chains):
            try:
                next(chain)
            except StopIteration:
                chains.remove(chain)
    for copy in loads.values():
        copy.wait()
    for copy in sent:
        copy.wait_send()
    for copy in stores:
        copy.wait()


def per_device(*args):
    any_space = pl.BlockSpec(memory_space=pl.ANY)
    shapes = (
        (1, 64, 1024),
        (1, 64, 768),
        (1, 96, 512),
        (1, 512, 128),
        (1, 384, 128),
        (384, 128),
    )
    scratch = [pltpu.VMEM(s, t) for part in (INPUTS, OUTPUTS, SCRATCH) for s, t in part.values()]
    scratch += [
        pltpu.SemaphoreType.DMA((N_REMOTE,)),
        pltpu.SemaphoreType.DMA((N_REMOTE,)),
        pltpu.SemaphoreType.DMA((N_LOCAL,)),
    ]
    args = list(args)
    for i in (10, 11):
        args[i] = jnp.swapaxes(args[i], 1, 2)
    outs = pl.pallas_call(
        body,
        out_shape=tuple(jax.ShapeDtypeStruct(s, F32) for s in shapes),
        in_specs=[any_space] * len(INPUTS),
        out_specs=(any_space,) * len(OUTPUTS),
        scratch_shapes=scratch,
        compiler_params=pltpu.CompilerParams(
            collective_id=0, has_side_effects=True, vmem_limit_bytes=63 * 1024 * 1024
        ),
    )(*args)
    return tuple(jnp.swapaxes(o, 1, 2) if i < 2 else o for i, o in enumerate(outs))


def solution(mesh):
    return jax.shard_map(
        per_device,
        mesh=mesh,
        in_specs=(
            P("sec", "col", "row"),
            P("sec", "row", "col"),
            P("sec", "col", "row"),
            P("sec", "row", "col"),
            P("col", ("sec", "row")),
            P(),
            P(),
            P("sec", "row", "col"),
            P("sec", "row", "col"),
            P(("sec", "row"), "col"),
            P("sec", "col", "row"),
            P("sec", "col", "row"),
            P("col", ("sec", "row"), None),
        ),
        out_specs=(
            P("sec", "col", "row"),
            P("sec", "col", "row"),
            P("col", ("sec", "row"), None),
            P("sec", "row", "col"),
            P("sec", "row", "col"),
            P(("sec", "row"), "col"),
        ),
        check_vma=False,
    )
```

time: 647 us -> 174 us (0.27)
  waiting for transfers between devices: 426 us -> 0 us
  Pallas kernels: 0 us -> 164 us
  blocking collectives: 100 us -> 0 us
  other arithmetic: 34.2 us -> 0 us
  matrix products: 29.3 us -> 0 us
  local copies, waits for them, and re-layouts: 33 us -> 8.91 us
  between operations: 15.7 us -> 0.66 us
  starting transfers between devices: 6.62 us -> 0 us
    reduce_scatter x11 -> x0, waiting for transfers between devices: 209 us -> none  [the longest x5 69.4 us: sum_cols(): return lax.psum_scatter(block, 'col', scatter_dimension=1, tiled=True)]
    pallas_call x0 -> x1, Pallas kernels: none -> 164 us  [per_device(): pl.pallas_call(body, out_shape=tuple((jax.ShapeDtypeStruct(s, F32) for s...]
    all_gather x5 -> x0, waiting for transfers between devices: 104 us -> none  [the longest x2 82.9 us: root_gather(): return lax.all_gather(block, ('sec', 'row'), axis=0, tiled=True)]
    all_gather x7 -> x0, blocking collectives: 100 us -> none  [the longest x5 52.6 us: spread_cols(): return lax.all_gather(block, 'col', axis=1, tiled=True)]
    unnamed x18 -> x0, waiting for transfers between devices: 80.8 us -> none
    ppermute x5 -> x0, waiting for transfers between devices: 32.4 us -> none  [from_partner(): lax.ppermute(x, axis, [(i, i ^ 1 << bit) for i in range(lax.axis_size(axi...]
    dot_general x10 -> x0, matrix products: 29.3 us -> none  [matmul(): return jnp.dot(left, right, preferred_element_type=jnp.float32)]
    convert_element_type x11 -> x0, other arithmetic: 16.5 us -> none  [the longest x1 4.24 us: per_device(): dense_root.astype(jnp.bfloat16)]
  transfers between devices with their start and end apart: 22 -> 0, of which waited for: 19 -> 0; matrix products, arithmetic and copies ran while one was open for 13% -> 0% of each run, Pallas kernels for 0% -> 0%
where the time goes in v1:
time: 174 us; the launch traced here: 173 us
  Pallas kernels  164 us (94%)
  local copies, waits for them, and re-layouts  8.91 us (5%)
    pallas_call x1, Pallas kernels, per_device(): pl.pallas_call(body, out_shape=tuple((jax.ShapeDtypeStruct(s, F32) for s...  164 us
    unnamed x8, local copies, waits for them, and re-layouts  8.91 us

profile of v1, /device:TPU:1, one launch (start us, length us, event | category | flops | bytes accessed | tf_op | source)
XLA Modules:
  0.0 173.4 jit_solution(6124109114613628365)
XLA Ops:
  0.6 163.9 %shard_map.172 = (f32[1,64,1024]{2,1,0:T(8,128)}, f32[1,64,768]{2,1,0:T(8,128)}, f32[1,96,512]{2,1,0:T(8,128)}, f32[1,512,128]{2,1,0:T(8,128)}, f32[1,384,128]{2,1,0:T(8,128)}, /*index=5*/f32[384,128]{1,0:T(8,128)}) custom-call(bf16[1,1024,512]{2,1,0:T(8,128)(2,1)} %refs_0_.1, bf16[1,256,1024]{2,1,0:T(8,128)(2,1)} %refs_1_.1, bf16[1,1536,384]{2,1,0:T(8,128)(2,1)} %refs_2_.1, ...), custom_call_target="tpu_custom_call" | custom-call | tf_op jit(solution)/shard_map/pallas_call | solution.py:741
  164.5 0.0 copy-start
  164.5 1.7 copy.25
  166.2 1.6 copy.26
  167.8 1.6 copy.27
  169.5 1.7 copy.28
  171.1 1.6 copy.29
  172.7 0.0 copy-done
  172.7 0.7 copy.30
Async XLA Ops:
  164.5 8.2 %copy-start = (f32[384,128]{1,0:T(8,128)S(1)}, f32[384,128]{1,0:T(8,128)}, u32[]{:S(2)}) copy-start(f32[384,128]{1,0:T(8,128)} %get-tuple-element.29) | copy-start | bytes 589828

commit v2 on v1

--- a/solution.py
+++ b/solution.py
@@ -49,24 +49,19 @@
     f_cs=((3, 256, 128), BF),
     f_cr=((3, 256, 128), BF),
     f_c=((2, 8, 256, 128), BF),
-    f_fc=((128, 128), F32),
     f_px=((4, 384, 128), BF),
     f_qs=((4, 768, 128), BF),
     f_k=((4, 768, 128), F32),
     f_qr=((4, 768, 128), BF),
-    f_qxs=((3, 768, 128), BF),
-    f_qxr=((3, 768, 128), BF),
-    f_q=((768, 128), F32),
-    f_qps=((384, 128), BF),
-    f_qpr=((384, 128), BF),
+    f_qxs=((7, 384, 128), BF),
+    f_qxr=((7, 384, 128), BF),
     f_pu=((384, 128), F32),
     f_pus=((384, 128), F32),
     f_x3=((4, 2, 384, 128), BF),
-    f_ds=((3, 256, 128), BF),
-    f_dr=((3, 256, 128), BF),
-    f_up=((2, 128, 128), F32),
-    f_ups=((128, 128), BF),
-    f_upr=((128, 128), BF),
+    f_ds=((7, 128, 128), BF),
+    f_dr=((7, 128, 128), BF),
+    f_uk=((4, 256, 128), F32),
+    f_fr=((512, 128), F32),
     f_r=((2, 8, 2, 128, 128), BF),
     f_rx=((4, 384, 128), BF),
     f_t=((2, 4, 4, 96, 512), BF),
@@ -104,10 +99,8 @@
     b_fx=((512, 128), BF),
     b_v=((2, 4, 2, 256, 128), BF),
     b_vr=((2, 4, 256, 128), BF),
-    b_vxs=((3, 2, 256, 128), BF),
-    b_vxr=((3, 2, 256, 128), BF),
-    b_vp=((2, 256, 128), BF),
-    b_vpr=((256, 128), BF),
+    b_vxs=((7, 256, 128), BF),
+    b_vxr=((7, 256, 128), BF),
     b_ck=((4, 256, 128), BF),
     b_ls=((4, 512, 128), BF),
     b_k=((4, 512, 128), F32),
@@ -119,7 +112,7 @@
     b_ms=((3, 512, 128), BF),
     b_mr=((3, 512, 128), BF),
 )
-N_REMOTE = 180
+N_REMOTE = 260
 N_LOCAL = len(INPUTS) + len(OUTPUTS)
 
 
@@ -159,8 +152,18 @@
     def at_z(d):
         return {"col": (z + d) % 4}
 
+    def at_xy(dx, dy):
+        return {"row": ((x + dx) % 4) * 2 + c, "sec": (sec + dy) % 4}
+
+    def at_px(d, q):
+        return {"row": ((x + d) % 4) * 2 + c, "sec": p * 2 + (oh if q else h)}
+
+    def at_pz(d, q):
+        return {"col": (z + d) % 4, "sec": p * 2 + (oh if q else h)}
+
     sibling = {"row": x * 2 + sib}
-    pair = {"sec": p * 2 + oh}
+    near = (0, 1, 3, 2)
+    eight = [(0, 1)] + [(d, q) for d in (1, 3, 2) for q in (0, 1)]
 
     loads = {}
     for i, (ref, src) in enumerate(zip(rest, hbm_in)):
@@ -188,7 +191,8 @@
         stores.append(copy)
 
     barrier = pltpu.get_barrier_semaphore()
-    peers = [sibling] + [f(d) for f in (at_x, at_y, at_z) for d in (1, 2, 3)]
+    peers = [sibling] + [at_z(d) for d in (1, 2, 3)] + [at_pz(d, 1) for d in (1, 2, 3)]
+    peers += [at_xy(dx, dy) for dx in range(4) for dy in range(4) if dx or dy]
     for peer in peers:
         pl.semaphore_signal(barrier, inc=1, device_id=peer, device_id_type=MESH)
     pl.semaphore_wait(barrier, len(peers))
@@ -233,6 +237,36 @@
 
         return wrap
 
+    def slot(d, q):
+        return 3 + d if q else d - 1
+
+    def tot7(part, m):
+        return tot(part, m) + (
+            (part[3, m, :].astype(F32) + part[4, m, :].astype(F32))
+            + (part[5, m, :].astype(F32) + part[6, m, :].astype(F32))
+        )
+
+    def hand_over(ref, got):
+        core = []
+        for d in near:
+            arrive(got[d])
+            part = ref((x + 4 - d) % 4)
+            core.append(send(part, part, sibling))
+        return core
+
+    def select(core, matrix, src, out):
+        rows = matrix.shape[0]
+        for i, d in enumerate(near):
+            core[i].wait_recv()
+            ch = (x + 4 - d) % 4
+            for q in range(2):
+                at = pl.ds(pl.multiple_of(q * 2048 + ch * 512, 512), 512)
+                r = dot(matrix[:, at], src[q, pl.ds(2 * ch, 2)].reshape(512, 128))
+                if i == 0 and q == 0:
+                    out[:rows, :] = r
+                else:
+                    out[:rows, :] = out[:rows, :] + r
+
     def build(ref, base_of, table, first):
         count = ref.shape[0]
 
@@ -257,11 +291,18 @@
             for j in range(4):
                 out[j, m, :] = r[:, j * 128 : (j + 1) * 128].astype(out.dtype)
 
-    def pick(matrix, vec, out):
-        @pl.loop(0, 8)
-        def _(k):
-            r = dot_t(matrix[:, pl.ds(pl.multiple_of(k * 512, 512), 512)], vec[...])
-            out[k // 4, lax.rem(k, 4)] = r.astype(BF).reshape(2, 256, 128)
+    def pick(matrix, vec, out, part):
+        core = []
+        for q in range(2):
+
+            @pl.loop(0, 4)
+            def _(k):
+                at = pl.multiple_of(q * 2048 + k * 512, 512)
+                r = dot_t(matrix[:, pl.ds(at, 512)], vec[...])
+                out[q, k] = r.astype(BF).reshape(2, 256, 128)
+
+            core.append(send(out.at[q, :, sib], part.at[q], sibling))
+        return core
 
     def hand_on(keep, part, buf, count):
         @tiles(count, 128)
@@ -339,31 +380,24 @@
         arrive(got)
         own = own + (v.f_cr[0].astype(F32) + v.f_cr[1].astype(F32)) + v.f_cr[2].astype(F32)
         v.f_c[h, row] = (-own).astype(BF)
-        got = send(v.f_c.at[h, row], v.f_c.at[h, row], pair)
+        got = {d: [] for d in near}
+        for d, q in eight:
+            got[d].append(send(v.f_c.at[h, row], v.f_c.at[h, row], at_px(d, q)))
         up.wait_recv()
         v.o_cu[:, pl.ds(pl.multiple_of(c * 512, 128), 512)] = lanes(v.f_u[...])
         v.o_cu[:, pl.ds(pl.multiple_of(sib * 512, 128), 512)] = lanes(v.f_us[...])
         emit(v.o_cu, 0)
         yield
-        got.wait_recv()
-        got = spread(v.f_c.at[:, row], at_x)
-        core = [send(v.f_c.at[:, row], v.f_c.at[:, row], sibling)]
-        yield
         need(v.i_pr)
-        for copy, d in zip(got, (1, 3, 2)):
-            copy.wait_recv()
-            ref = v.f_c.at[:, ((x + 4 - d) % 4) * 2 + c]
-            core.append(send(ref, ref, sibling))
-        yield
-        arrive(core)
+        core = hand_over(lambda k: v.f_c.at[:, 2 * k + c], got)
+        yield
+        select(core, v.sel, v.f_c, v.f_fr)
 
         @tiles(384, 128)
         def _(m):
-            front = dot(v.sel[m, :], v.f_c[...].reshape(4096, 128))
-            v.f_px[z, m, :] = (v.i_pr[m, :] + front).astype(BF)
+            v.f_px[z, m, :] = (v.i_pr[m, :] + v.f_fr[m, :]).astype(BF)
 
         got = spread(v.f_px.at[z], at_z)
-        v.f_fc[...] = dot(v.sel[384:, :], v.f_c[...].reshape(4096, 128))
         yield
         need(v.wpi)
         core = []
@@ -382,27 +416,24 @@
         yield
         arrive(core)
         got = []
-        for d in (1, 3, 2):
+        for d, q in eight[1:] + eight[:1]:
             ch = (x + d) % 4
-            hand_on(v.f_k.at[ch], v.f_qr.at[ch], v.f_qxs.at[d - 1], 768)
-            got.append(send(v.f_qxs.at[d - 1], v.f_qxr.at[d - 1], at_x(d)))
-        yield
-        arrive(got)
-
-        @tiles(768, 128)
-        def _(m):
-            own = v.f_k[x, m, :] + v.f_qr[x, m, :].astype(F32)
-            v.f_q[m, :] = own + tot(v.f_qxr, m)
-
-        v.f_qps[...] = v.f_q[pl.ds(oh * 384, 384), :].astype(BF)
-        got = send(v.f_qps, v.f_qpr, pair)
-        yield
-        got.wait_recv()
-        own = v.f_q[pl.ds(h * 384, 384), :] + v.f_qpr[...].astype(F32)
-        v.f_x3[x, c] = own.astype(BF)
+            at = pl.ds(pl.multiple_of((oh if q else h) * 384, 128), 384)
+            buf = v.f_qxs.at[slot(d, q)]
+            hand_on(v.f_k.at[ch, at], v.f_qr.at[ch, at], buf, 384)
+            got.append(send(buf, v.f_qxr.at[slot(d, q)], at_px(d, q)))
+        yield
+        arrive(got)
+
+        @tiles(384, 128)
+        def _(m):
+            at = pl.ds(pl.multiple_of(h * 384 + m.start, 128), 128)
+            own = v.f_k[x, at, :] + v.f_qr[x, at, :].astype(F32) + tot7(v.f_qxr, m)
+            v.f_pu[m, :] = own
+            v.f_x3[x, c, m, :] = own.astype(BF)
+
         got = spread(v.f_x3.at[x, c], at_x)
         core = [send(v.f_x3.at[x, c], v.f_x3.at[x, c], sibling)]
-        v.f_pu[...] = own
         up = send(v.f_pu, v.f_pus, sibling)
         yield
         need(v.wpl)
@@ -413,100 +444,100 @@
         yield
         arrive(core)
         got = []
-        for d in (1, 3, 2):
+        for d in (1, 3, 2, 0):
             ch = (z + d) % 4
-            r = dot(v.wpl[...], v.f_x3[ch].reshape(768, 128))
-            v.f_ds[d - 1] = r.astype(BF)
-            got.append(send(v.f_ds.at[d - 1], v.f_dr.at[d - 1], at_z(d)))
-        own = dot(v.wpl[...], v.f_x3[z].reshape(768, 128))
-        yield
-        arrive(got)
-        own = own + (v.f_dr[0].astype(F32) + v.f_dr[1].astype(F32)) + v.f_dr[2].astype(F32)
-        v.f_up[...] = own.reshape(2, 128, 128)
-        v.f_ups[...] = v.f_up[oh].astype(BF)
-        got = send(v.f_ups, v.f_upr, pair)
+            v.f_uk[ch] = dot(v.wpl[...], v.f_x3[ch].reshape(768, 128))
+            for q in (0, 1):
+                if d or q:
+                    at = pl.ds(pl.multiple_of((oh if q else h) * 128, 128), 128)
+                    v.f_ds[slot(d, q)] = v.f_uk[ch, at, :].astype(BF)
+                    got.append(send(v.f_ds.at[slot(d, q)], v.f_dr.at[slot(d, q)], at_pz(d, q)))
         up.wait_recv()
         v.o_pu[:, pl.ds(pl.multiple_of(c * 384, 128), 384)] = lanes(v.f_pu[...])
         v.o_pu[:, pl.ds(pl.multiple_of(sib * 384, 128), 384)] = lanes(v.f_pus[...])
         emit(v.o_pu, 1)
         yield
-        got.wait_recv()
-        own = v.f_fc[...] - (v.f_up[h] + v.f_upr[...].astype(F32))
-        v.f_r[p, row, h] = own.astype(BF)
-        got = spread(v.f_r.at[p, row, h], at_y)
-        yield
-        arrive(got)
-        got = spread(v.f_r.at[:, row], at_x)
-        core = [send(v.f_r.at[:, row], v.f_r.at[:, row], sibling)]
+        arrive(got)
+        own = v.f_uk[z, pl.ds(h * 128, 128), :] + tot7(v.f_dr, slice(None))
+        v.f_r[p, row, h] = (v.f_fr[384:, :] - own).astype(BF)
+        got = {d: [] for d in near}
+        for dx in near:
+            for dy in near:
+                if dx or dy:
+                    ref = v.f_r.at[p, row, h]
+                    got[dx].append(send(ref, ref, at_xy(dx, dy)))
         yield
         need(v.i_rr)
-        for copy, d in zip(got, (1, 3, 2)):
-            copy.wait_recv()
-            ref = v.f_r.at[:, ((x + 4 - d) % 4) * 2 + c]
-            core.append(send(ref, ref, sibling))
-        yield
-        arrive(core)
+        core = hand_over(lambda k: v.f_r.at[:, 2 * k + c], got)
+        yield
+        select(core, v.rsel, v.f_r, v.f_fr)
 
         @tiles(384, 128)
         def _(m):
-            front = dot(v.rsel[m, :], v.f_r[...].reshape(4096, 128))
-            v.f_rx[z, m, :] = (v.i_rr[m, :] + front).astype(BF)
+            v.f_rx[z, m, :] = (v.i_rr[m, :] + v.f_fr[m, :]).astype(BF)
 
         got = spread(v.f_rx.at[z], at_z)
         yield
         arrive(got)
         core = []
-        for s in range(4):
-
-            @pl.loop(0, 4)
+        for dy in (1, 3, 2, 0):
+            s = (sec + dy) % 4
+
+            @pl.loop(0, 2)
             def _(k):
-                start = pl.multiple_of((s * 4 + k) * 192, 192)
-                r = dot(v.wr[pl.ds(start, 192), :], wide(v.f_rx, 384))
-                v.f_t[0, s, k] = r[:96].astype(BF)
-                v.f_t[1, s, k] = r[96:].astype(BF)
+                start = pl.multiple_of(s * 768 + k * 384, 384)
+                r = dot(v.wr[pl.ds(start, 384), :], wide(v.f_rx, 384))
+                for j in range(2):
+                    for cc in range(2):
+                        at = (2 * j + cc) * 96
+                        v.f_t[cc, s, 2 * k + j] = r[at : at + 96].astype(BF)
 
             core.append(send(v.f_t.at[sib, s], v.f_tr.at[s], sibling))
         yield
-        arrive(core)
         got_a, got_b = [], []
-        for d in (1, 3, 2):
-            ch = (x + d) % 4
-
-            @pl.loop(0, 4)
-            def _(s):
-                v.f_as[d - 1, s] = root_sum(s, ch, 0).astype(BF)
-
-            got_a.append(send(v.f_as.at[d - 1], v.f_ar.at[d - 1], at_x(d)))
-            cy = (sec + d) % 4
-
-            @pl.loop(0, 4)
-            def _(s):
-                v.f_bs[d - 1, s] = root_sum(cy, s, 256).astype(BF)
-
-            got_b.append(send(v.f_bs.at[d - 1], v.f_br.at[d - 1], at_y(d)))
-
-        @pl.loop(0, 4)
-        def _(s):
+        for i, dy in enumerate((1, 3, 2, 0)):
+            s = (sec + dy) % 4
+            core[i].wait_recv()
+            if dy:
+
+                @pl.loop(0, 4)
+                def _(k):
+                    v.f_bs[dy - 1, k] = root_sum(s, k, 256).astype(BF)
+
+                got_b.append(send(v.f_bs.at[dy - 1], v.f_br.at[dy - 1], at_y(dy)))
+            else:
+
+                @pl.loop(0, 4)
+                def _(k):
+                    v.f_ob[k] = root_sum(s, k, 256)
+
+            part = []
+            for d in (1, 3, 2):
+                v.f_as[d - 1, s] = root_sum(s, (x + d) % 4, 0).astype(BF)
+                part.append(send(v.f_as.at[d - 1, s], v.f_ar.at[d - 1, s], at_x(d)))
+            got_a.append(part)
             v.f_oa[s] = root_sum(s, x, 0)
-            v.f_ob[s] = root_sum(sec, s, 256)
-
-        yield
-        for got, total, part in ((got_a, v.f_oa, v.f_ar), (got_b, v.f_ob, v.f_br)):
-            arrive(got)
-
-            @pl.loop(0, 4)
-            def _(s):
-                total[s] = total[s] + (
-                    (part[0, s].astype(F32) + part[1, s].astype(F32))
-                    + part[2, s].astype(F32)
-                )
-
-        got = []
-        for d in (1, 3, 2):
-            v.f_a2s[d - 1] = v.f_oa[(sec + d) % 4].astype(BF)
-            got.append(send(v.f_a2s.at[d - 1], v.f_a2r.at[d - 1], at_y(d)))
-            v.f_b2s[d - 1] = v.f_ob[(x + d) % 4].astype(BF)
+        yield
+
+        def gathered(total, part, k):
+            return total[k] + (
+                (part[0, k].astype(F32) + part[1, k].astype(F32)) + part[2, k].astype(F32)
+            )
+
+        got = []
+        for i, dy in enumerate((1, 3, 2, 0)):
+            s = (sec + dy) % 4
+            arrive(got_a[i])
+            if dy:
+                v.f_a2s[dy - 1] = gathered(v.f_oa, v.f_ar, s).astype(BF)
+                got.append(send(v.f_a2s.at[dy - 1], v.f_a2r.at[dy - 1], at_y(dy)))
+            else:
+                v.f_oa[s] = gathered(v.f_oa, v.f_ar, s)
+        arrive(got_b)
+        for d in (1, 3, 2):
+            v.f_b2s[d - 1] = gathered(v.f_ob, v.f_br, (x + d) % 4).astype(BF)
             got.append(send(v.f_b2s.at[d - 1], v.f_b2r.at[d - 1], at_x(d)))
+        v.f_ob[x] = gathered(v.f_ob, v.f_br, x)
         yield
         arrive(got)
         for total, me, part, lo in ((v.f_oa, sec, v.f_a2r, 0), (v.f_ob, x, v.f_b2r, 256)):
@@ -518,34 +549,40 @@
     def backward():
         need(v.i_rb)
         v.b_y[sec, x, c] = v.i_rb[...].astype(BF)
-        ref_a = v.b_y.at[sec, x, c, :, 0:256]
-        ref_b = v.b_y.at[sec, x, c, :, 256:512]
-        got_a = spread(ref_a, at_x)
-        got_b = spread(ref_b, at_y)
+        got_x = spread(v.b_y.at[sec, x, c], at_x)
+        got_y = spread(v.b_y.at[sec, x, c], at_y)
         need(v.i_cb, v.i_pb)
         cbs = send(v.i_cb, v.b_cbs, sibling)
         pbs = send(v.i_pb, v.b_pbs, sibling)
         yield
         need(v.pmap)
         build(v.rsel, root_base, v.pmap, 0)
-        arrive(got_a)
-        got = spread(v.b_y.at[sec, :, c, :, 0:256], at_y)
-        arrive(got_b)
-        got += spread(v.b_y.at[:, x, c, :, 256:512], at_x)
-        yield
-        arrive(got)
-        core = [send(v.b_y.at[s, :, c], v.b_y.at[s, :, c], sibling) for s in range(4)]
+        got_a, got_b = [], []
+        for i, d in enumerate((1, 3, 2)):
+            got_x[i].wait_recv()
+            got_a.append(spread(v.b_y.at[sec, (x + 4 - d) % 4, c, :, 0:256], at_y))
+            got_y[i].wait_recv()
+            got_b.append(spread(v.b_y.at[(sec + 4 - d) % 4, x, c, :, 256:512], at_x))
+        core = [send(v.b_y.at[sec, :, c], v.b_y.at[sec, :, c], sibling)]
+        yield
+        for i, d in enumerate((1, 3, 2)):
+            arrive([part[i] for part in got_a])
+            arrive(got_b[i])
+            ref = v.b_y.at[(sec + 4 - d) % 4, :, c]
+            core.append(send(ref, ref, sibling))
         need(v.wr)
         yield
-        for s in range(4):
-            core[s].wait_recv()
+        for i, d in enumerate(near):
+            core[i].wait_recv()
+            s = (sec + 4 - d) % 4
 
             @tiles(384, 128)
             def _(m):
-                r = dot_t(v.wr[s * 768 : (s + 1) * 768, m], v.b_y[s].reshape(768, 512))
+                w = v.wr[pl.ds(pl.multiple_of(s * 768, 768), 768), m]
+                r = dot_t(w, v.b_y[s].reshape(768, 512))
                 for j in range(4):
                     part = r[:, j * 128 : (j + 1) * 128]
-                    v.b_r[j, m, :] = part if s == 0 else v.b_r[j, m, :] + part
+                    v.b_r[j, m, :] = part if i == 0 else v.b_r[j, m, :] + part
 
         got = []
         for d in (1, 3, 2):
@@ -561,10 +598,9 @@
             v.b_rx[m, :] = own.astype(BF)
 
         emit(v.o_rx, 5)
-        pick(v.rsel, v.b_rx, v.b_t)
-        core = send(v.b_t.at[:, :, sib], v.b_tr, sibling)
-        yield
-        core.wait_recv()
+        core = pick(v.rsel, v.b_rx, v.b_t, v.b_tr)
+        yield
+        arrive(core)
         got = []
         for d in (1, 3, 2):
             ch = (x + d) % 4
@@ -607,17 +643,12 @@
             own = both(v.i_pb[:, at], v.b_pbs[:, at]) - (own + tot(v.b_exr, m))
             v.b_g[x, h, c, m, :] = own.astype(BF)
 
-        got = send(v.b_g.at[x, h, c], v.b_g.at[x, h, c], pair)
-        yield
-        got.wait_recv()
-        got = spread(v.b_g.at[x, :, c], at_x)
-        core = [send(v.b_g.at[x, :, c], v.b_g.at[x, :, c], sibling)]
+        got = {d: [] for d in near}
+        for d, q in eight:
+            got[d].append(send(v.b_g.at[x, h, c], v.b_g.at[x, h, c], at_px(d, q)))
         yield
         need(v.wpi)
-        for copy, d in zip(got, (1, 3, 2)):
-            copy.wait_recv()
-            ref = v.b_g.at[(x + 4 - d) % 4, :, c]
-            core.append(send(ref, ref, sibling))
+        core = hand_over(lambda k: v.b_g.at[k, :, c], got)
         yield
         arrive(core)
         back_mm(v.wpi, 0, v.b_g, 1536, v.b_r)
@@ -636,25 +667,20 @@
 
         emit(v.o_px, 4)
         v.b_fx[384:, :] = v.b_pk[z, pl.ds(h * 128, 128), :]
-        pick(v.sel, v.b_fx, v.b_v)
-        core = send(v.b_v.at[:, :, sib], v.b_vr, sibling)
-        yield
-        core.wait_recv()
-        got = []
-        for d in (1, 3, 2):
+        core = pick(v.sel, v.b_fx, v.b_v, v.b_vr)
+        yield
+        arrive(core)
+        got = []
+        for d, q in eight[1:] + eight[:1]:
             ch = (x + d) % 4
-            for q in range(2):
-                v.b_vxs[d - 1, q] = v.b_v[q, ch, c] + v.b_vr[q, ch]
-            got.append(send(v.b_vxs.at[d - 1], v.b_vxr.at[d - 1], at_x(d)))
-        yield
-        arrive(got)
-        for q in range(2):
-            own = v.b_v[q, x, c] + v.b_vr[q, x]
-            v.b_vp[q] = own + ((v.b_vxr[0, q] + v.b_vxr[1, q]) + v.b_vxr[2, q])
-        got = send(v.b_vp.at[oh], v.b_vpr, pair)
-        yield
-        got.wait_recv()
-        v.b_ck[z] = v.b_vp[h] + v.b_vpr[...]
+            a = oh if q else h
+            v.b_vxs[slot(d, q)] = v.b_v[a, ch, c] + v.b_vr[a, ch]
+            got.append(send(v.b_vxs.at[slot(d, q)], v.b_vxr.at[slot(d, q)], at_px(d, q)))
+        yield
+        arrive(got)
+        own = v.b_v[h, x, c] + v.b_vr[h, x] + (v.b_vxr[0] + v.b_vxr[1] + v.b_vxr[2])
+        own = own + ((v.b_vxr[3] + v.b_vxr[4]) + (v.b_vxr[5] + v.b_vxr[6]))
+        v.b_ck[z] = own
         got = spread(v.b_ck.at[z], at_z)
         yield
         need(v.wcl)
@@ -716,6 +742,17 @@
     for copy in sent:
         copy.wait_send()
     for copy in stores:
+        copy.wait()
+
+
+def write_out(*refs):
+    n = len(OUTPUTS)
+    copies = [
+        pltpu.make_async_copy(refs[i], refs[n + i], refs[2 * n].at[i]) for i in range(n)
+    ]
+    for copy in copies:
+        copy.start()
+    for copy in copies:
         copy.wait()
 
 
@@ -748,6 +785,13 @@
             collective_id=0, has_side_effects=True, vmem_limit_bytes=63 * 1024 * 1024
         ),
     )(*args)
+    outs = pl.pallas_call(
+        write_out,
+        out_shape=tuple(jax.ShapeDtypeStruct(s, F32) for s in shapes),
+        in_specs=[any_space] * len(OUTPUTS),
+        out_specs=(any_space,) * len(OUTPUTS),
+        scratch_shapes=[pltpu.SemaphoreType.DMA((len(OUTPUTS),))],
+    )(*outs)
     return tuple(jnp.swapaxes(o, 1, 2) if i < 2 else o for i, o in enumerate(outs))
 
 

time: 174 us -> 202 us (1.16); the launches traced: 173 us -> 198 us
  Pallas kernels: 164 us -> 198 us
  local copies, waits for them, and re-layouts: 8.91 us -> 0 us
    pallas_call x0 -> x1, Pallas kernels: none -> 40.9 us  [per_device(): pl.pallas_call(write_out, out_shape=tuple((jax.ShapeDtypeStruct(s, F32) f...]
    unnamed x8 -> x0, local copies, waits for them, and re-layouts: 8.91 us -> none
    pallas_call x1, Pallas kernels: 164 us -> 157 us  [per_device(): pl.pallas_call(body, out_shape=tuple((jax.ShapeDtypeStruct(s, F32) for s...]
where the time goes in v2:
time: 202 us; the launch traced here: 198 us
  Pallas kernels  198 us (98%)
    pallas_call x1, Pallas kernels, per_device(): pl.pallas_call(body, out_shape=tuple((jax.ShapeDtypeStruct(s, F32) for s...  157 us
    pallas_call x1, Pallas kernels, per_device(): pl.pallas_call(write_out, out_shape=tuple((jax.ShapeDtypeStruct(s, F32) f...  40.9 us

profile of v2, /device:TPU:1, one launch (start us, length us, event | category | flops | bytes accessed | tf_op | source)
XLA Modules:
  0.0 198.3 jit_solution(15367582932768593024)
XLA Ops:
  0.6 156.7 %shard_map.172 = (f32[1,64,1024]{2,1,0:T(8,128)}, f32[1,64,768]{2,1,0:T(8,128)}, f32[1,96,512]{2,1,0:T(8,128)}, f32[1,512,128]{2,1,0:T(8,128)}, f32[1,384,128]{2,1,0:T(8,128)}, /*index=5*/f32[384,128]{1,0:T(8,128)}) custom-call(bf16[1,1024,512]{2,1,0:T(8,128)(2,1)} %refs_0_.1, bf16[1,256,1024]{2,1,0:T(8,128)(2,1)} %refs_1_.1, bf16[1,1536,384]{2,1,0:T(8,128)(2,1)} %refs_2_.1, ...), custom_call_target="tpu_custom_call" | custom-call | tf_op jit(solution)/shard_map/pallas_call | solution.py:778
  157.3 40.9 %shard_map.173 = (f32[1,64,1024]{2,1,0:T(8,128)}, f32[1,64,768]{2,1,0:T(8,128)}, f32[1,96,512]{2,1,0:T(8,128)}, f32[1,512,128]{2,1,0:T(8,128)}, f32[1,384,128]{2,1,0:T(8,128)}, /*index=5*/f32[384,128]{1,0:T(8,128)}) custom-call(f32[1,64,1024]{2,1,0:T(8,128)} %get-tuple-element.18.refs_0_, f32[1,64,768]{2,1,0:T(8,128)} %get-tuple-element.19.refs_1_, ...), custom_call_target="tpu_custom_call" | custom-call | tf_op jit(solution)/shard_map/pallas_call | solution.py:788

commit v3 on v2

--- a/solution.py
+++ b/solution.py
@@ -93,6 +93,7 @@
     b_exs=((3, 384, 128), BF),
     b_exr=((3, 384, 128), BF),
     b_pbs=((64, 768), F32),
+    b_pb=((384, 128), F32),
     b_g=((4, 2, 2, 384, 128), BF),
     b_hs=((3, 384, 128), BF),
     b_hr=((3, 384, 128), BF),
@@ -108,11 +109,13 @@
     b_lxs=((3, 512, 128), BF),
     b_lxr=((3, 512, 128), BF),
     b_cbs=((64, 1024), F32),
+    b_cb=((512, 128), F32),
     b_h=((4, 2, 512, 128), BF),
     b_ms=((3, 512, 128), BF),
     b_mr=((3, 512, 128), BF),
 )
-N_REMOTE = 260
+N_REMOTE = 320
+ORDER = "BFBFBFBFBBFFBFBBFBFBFFBBFBFFBFBBFBFBFFBBFBF"
 N_LOCAL = len(INPUTS) + len(OUTPUTS)
 
 
@@ -254,6 +257,36 @@
             core.append(send(part, part, sibling))
         return core
 
+    def exchange(targets, buf, land, finish, home, onward, core):
+        size = home.shape[0] // 2
+        tile = 128 if size % 128 == 0 else 96
+        first, found = [], []
+        for half in range(2):
+            at = pl.ds(half * size, size)
+            got = []
+            for k, keep, part, peer in targets:
+                hand_on(keep.at[at], part.at[at], buf.at[k, at], size)
+                got.append(send(buf.at[k, at], land.at[k, at], peer))
+            first.append(got)
+        yield
+        for half in range(2):
+            at = pl.ds(half * size, size)
+            arrive(first[half])
+
+            @tiles(size, tile)
+            def _(m):
+                finish(pl.ds(pl.multiple_of(half * size + m.start, tile), tile))
+
+            ref = home.at[at]
+            for peer, where in onward:
+                found.append((send(ref, ref, peer), where.at[at]))
+            core.append(send(ref, ref, sibling))
+        yield
+        for copy, where in found:
+            copy.wait_recv()
+            core.append(send(where, where, sibling))
+        yield
+
     def select(core, matrix, src, out):
         rows = matrix.shape[0]
         for i, d in enumerate(near):
@@ -284,12 +317,10 @@
         return jnp.concatenate(parts, axis=1)
 
     def back_mm(w, start, src, depth, out):
-        @tiles(out.shape[1], 128)
-        def _(m):
-            at = pl.ds(pl.multiple_of(start + m.start, 128), 128)
-            r = dot_t(w[:, at], wide(src, depth))
-            for j in range(4):
-                out[j, m, :] = r[:, j * 128 : (j + 1) * 128].astype(out.dtype)
+        at = pl.ds(pl.multiple_of(start, 128), out.shape[1])
+        r = dot_t(w[:, at], wide(src, depth))
+        for j in range(4):
+            out[j] = r[:, j * 128 : (j + 1) * 128].astype(out.dtype)
 
     def pick(matrix, vec, out, part):
         core = []
@@ -305,7 +336,7 @@
         return core
 
     def hand_on(keep, part, buf, count):
-        @tiles(count, 128)
+        @tiles(count, 128 if count % 128 == 0 else 96)
         def _(m):
             buf[m, :] = (keep[m, :] + part[m, :].astype(F32)).astype(BF)
 
@@ -344,30 +375,27 @@
             v.f_k[ch, :512] = dot(v.wci[pl.ds(c * 512, 512), :], v.f_x[ch])
         yield
         arrive(core)
-        got = []
-        for d in (1, 3, 2):
-            ch = (x + d) % 4
-            hand_on(v.f_k.at[ch], v.f_pr.at[ch], v.f_xs.at[d - 1], 512)
-            got.append(send(v.f_xs.at[d - 1], v.f_xr.at[d - 1], at_x(d)))
-        yield
-        arrive(got)
-
-        @tiles(512, 128)
-        def _(m):
+
+        def finish(m):
             own = (v.f_k[x, m, :] + v.f_pr[x, m, :].astype(F32)) + tot(v.f_xr, m)
             v.f_x2[x, c, m, :] = own.astype(BF)
             v.f_u[m, :] = own
 
-        got = spread(v.f_x2.at[x, c], at_x)
-        core = [send(v.f_x2.at[x, c], v.f_x2.at[x, c], sibling)]
+        core = []
+        yield from exchange(
+            [
+                (d - 1, v.f_k.at[(x + d) % 4], v.f_pr.at[(x + d) % 4], at_x(d))
+                for d in (1, 3, 2)
+            ],
+            v.f_xs,
+            v.f_xr,
+            finish,
+            v.f_x2.at[x, c],
+            [(at_x(d), v.f_x2.at[(x + 4 - d) % 4, c]) for d in (1, 3, 2)],
+            core,
+        )
         up = send(v.f_u, v.f_us, sibling)
-        yield
         need(v.wcl)
-        for copy, d in zip(got, (1, 3, 2)):
-            copy.wait_recv()
-            ref = v.f_x2.at[(x + 4 - d) % 4, c]
-            core.append(send(ref, ref, sibling))
-        yield
         arrive(core)
         got = []
         for d in (1, 3, 2):
@@ -415,33 +443,30 @@
                 v.f_k[ch, half * 384 : (half + 1) * 384] = dot(w, v.f_px[ch])
         yield
         arrive(core)
-        got = []
+
+        def finish(m):
+            at = pl.ds(pl.multiple_of(h * 384 + m.start, 32), m.size)
+            own = v.f_k[x, at, :] + v.f_qr[x, at, :].astype(F32) + tot7(v.f_qxr, m)
+            v.f_pu[m, :] = own
+            v.f_x3[x, c, m, :] = own.astype(BF)
+
+        core = []
+        targets = []
         for d, q in eight[1:] + eight[:1]:
             ch = (x + d) % 4
             at = pl.ds(pl.multiple_of((oh if q else h) * 384, 128), 384)
-            buf = v.f_qxs.at[slot(d, q)]
-            hand_on(v.f_k.at[ch, at], v.f_qr.at[ch, at], buf, 384)
-            got.append(send(buf, v.f_qxr.at[slot(d, q)], at_px(d, q)))
-        yield
-        arrive(got)
-
-        @tiles(384, 128)
-        def _(m):
-            at = pl.ds(pl.multiple_of(h * 384 + m.start, 128), 128)
-            own = v.f_k[x, at, :] + v.f_qr[x, at, :].astype(F32) + tot7(v.f_qxr, m)
-            v.f_pu[m, :] = own
-            v.f_x3[x, c, m, :] = own.astype(BF)
-
-        got = spread(v.f_x3.at[x, c], at_x)
-        core = [send(v.f_x3.at[x, c], v.f_x3.at[x, c], sibling)]
+            targets.append((slot(d, q), v.f_k.at[ch, at], v.f_qr.at[ch, at], at_px(d, q)))
+        yield from exchange(
+            targets,
+            v.f_qxs,
+            v.f_qxr,
+            finish,
+            v.f_x3.at[x, c],
+            [(at_x(d), v.f_x3.at[(x + 4 - d) % 4, c]) for d in (1, 3, 2)],
+            core,
+        )
         up = send(v.f_pu, v.f_pus, sibling)
-        yield
         need(v.wpl)
-        for copy, d in zip(got, (1, 3, 2)):
-            copy.wait_recv()
-            ref = v.f_x3.at[(x + 4 - d) % 4, c]
-            core.append(send(ref, ref, sibling))
-        yield
         arrive(core)
         got = []
         for d in (1, 3, 2, 0):
@@ -576,13 +601,11 @@
             core[i].wait_recv()
             s = (sec + 4 - d) % 4
 
-            @tiles(384, 128)
-            def _(m):
-                w = v.wr[pl.ds(pl.multiple_of(s * 768, 768), 768), m]
-                r = dot_t(w, v.b_y[s].reshape(768, 512))
-                for j in range(4):
-                    part = r[:, j * 128 : (j + 1) * 128]
-                    v.b_r[j, m, :] = part if i == 0 else v.b_r[j, m, :] + part
+            w = v.wr[pl.ds(pl.multiple_of(s * 768, 768), 768), :]
+            r = dot_t(w, v.b_y[s].reshape(768, 512))
+            for j in range(4):
+                part = r[:, j * 128 : (j + 1) * 128]
+                v.b_r[j] = part if i == 0 else v.b_r[j] + part
 
         got = []
         for d in (1, 3, 2):
@@ -627,29 +650,32 @@
         back_mm(v.wpl, c * 384, v.b_pk, 256, v.b_k.at[:, :384])
         yield
         arrive(core)
-        got = []
-        for d in (1, 3, 2):
-            ch = (x + d) % 4
-            hand_on(v.b_k.at[ch], v.b_er.at[ch], v.b_exs.at[d - 1], 384)
-            got.append(send(v.b_exs.at[d - 1], v.b_exr.at[d - 1], at_x(d)))
-        yield
+
+        def finish(m):
+            own = v.b_k[x, m, :] + v.b_er[x, m, :].astype(F32)
+            own = v.b_pb[m, :] - (own + tot(v.b_exr, m))
+            v.b_g[x, h, c, m, :] = own.astype(BF)
+
+        core = []
         pbs.wait_recv()
-        arrive(got)
-
-        @tiles(384, 128)
-        def _(m):
-            at = pl.ds(pl.multiple_of(c * 384 + m.start, 128), 128)
-            own = v.b_k[x, m, :] + v.b_er[x, m, :].astype(F32)
-            own = both(v.i_pb[:, at], v.b_pbs[:, at]) - (own + tot(v.b_exr, m))
-            v.b_g[x, h, c, m, :] = own.astype(BF)
-
-        got = {d: [] for d in near}
-        for d, q in eight:
-            got[d].append(send(v.b_g.at[x, h, c], v.b_g.at[x, h, c], at_px(d, q)))
-        yield
+        at = pl.ds(pl.multiple_of(c * 384, 128), 384)
+        v.b_pb[...] = both(v.i_pb[:, at], v.b_pbs[:, at])
+        yield from exchange(
+            [
+                (d - 1, v.b_k.at[(x + d) % 4, :384], v.b_er.at[(x + d) % 4], at_x(d))
+                for d in (1, 3, 2)
+            ],
+            v.b_exs,
+            v.b_exr,
+            finish,
+            v.b_g.at[x, h, c],
+            [
+                (at_px(d, q), v.b_g.at[(x + 4 - d) % 4, oh if q else h, c])
+                for d, q in eight[1:] + eight[:1]
+            ],
+            core,
+        )
         need(v.wpi)
-        core = hand_over(lambda k: v.b_g.at[k, :, c], got)
-        yield
         arrive(core)
         back_mm(v.wpi, 0, v.b_g, 1536, v.b_r)
         got = []
@@ -690,31 +716,29 @@
         back_mm(v.wcl, c * 512, v.b_ck, 256, v.b_k)
         yield
         arrive(core)
-        got = []
-        for d in (1, 3, 2):
-            ch = (x + d) % 4
-            hand_on(v.b_k.at[ch], v.b_lr.at[ch], v.b_lxs.at[d - 1], 512)
-            got.append(send(v.b_lxs.at[d - 1], v.b_lxr.at[d - 1], at_x(d)))
-        yield
+
+        def finish(m):
+            own = v.b_k[x, m, :] + v.b_lr[x, m, :].astype(F32)
+            own = v.b_cb[m, :] - (own + tot(v.b_lxr, m))
+            v.b_h[x, c, m, :] = own.astype(BF)
+
+        core = []
         cbs.wait_recv()
-        arrive(got)
-
-        @tiles(512, 128)
-        def _(m):
-            at = pl.ds(pl.multiple_of(c * 512 + m.start, 128), 128)
-            own = v.b_k[x, m, :] + v.b_lr[x, m, :].astype(F32)
-            own = both(v.i_cb[:, at], v.b_cbs[:, at]) - (own + tot(v.b_lxr, m))
-            v.b_h[x, c, m, :] = own.astype(BF)
-
-        got = spread(v.b_h.at[x, c], at_x)
-        core = [send(v.b_h.at[x, c], v.b_h.at[x, c], sibling)]
-        yield
+        at = pl.ds(pl.multiple_of(c * 512, 128), 512)
+        v.b_cb[...] = both(v.i_cb[:, at], v.b_cbs[:, at])
+        yield from exchange(
+            [
+                (d - 1, v.b_k.at[(x + d) % 4], v.b_lr.at[(x + d) % 4], at_x(d))
+                for d in (1, 3, 2)
+            ],
+            v.b_lxs,
+            v.b_lxr,
+            finish,
+            v.b_h.at[x, c],
+            [(at_x(d), v.b_h.at[(x + 4 - d) % 4, c]) for d in (1, 3, 2)],
+            core,
+        )
         need(v.wci)
-        for copy, d in zip(got, (1, 3, 2)):
-            copy.wait_recv()
-            ref = v.b_h.at[(x + 4 - d) % 4, c]
-            core.append(send(ref, ref, sibling))
-        yield
         arrive(core)
         back_mm(v.wci, 0, v.b_h, 1024, v.b_k)
         got = []
@@ -730,13 +754,13 @@
 
         emit(v.o_cx, 3)
 
-    chains = [backward(), forward()]
-    while chains:
-        for chain in list(chains):
+    chains = dict(B=backward(), F=forward())
+    for name in ORDER + "BF" * 60:
+        if name in chains:
             try:
-                next(chain)
+                next(chains[name])
             except StopIteration:
-                chains.remove(chain)
+                del chains[name]
     for copy in loads.values():
         copy.wait()
     for copy in sent:
@@ -747,13 +771,16 @@
 
 def write_out(*refs):
     n = len(OUTPUTS)
-    copies = [
-        pltpu.make_async_copy(refs[i], refs[n + i], refs[2 * n].at[i]) for i in range(n)
-    ]
-    for copy in copies:
+    stage, sems = refs[2 * n : 3 * n], refs[3 * n]
+    loads = [pltpu.make_async_copy(refs[i], stage[i], sems.at[0, i]) for i in range(n)]
+    for copy in loads:
         copy.start()
-    for copy in copies:
-        copy.wait()
+    stores = [pltpu.make_async_copy(stage[i], refs[n + i], sems.at[1, i]) for i in range(n)]
+    for load, store in zip(loads, stores):
+        load.wait()
+        store.start()
+    for store in stores:
+        store.wait()
 
 
 def per_device(*args):
@@ -790,7 +817,8 @@
         out_shape=tuple(jax.ShapeDtypeStruct(s, F32) for s in shapes),
         in_specs=[any_space] * len(OUTPUTS),
         out_specs=(any_space,) * len(OUTPUTS),
-        scratch_shapes=[pltpu.SemaphoreType.DMA((len(OUTPUTS),))],
+        scratch_shapes=[pltpu.VMEM(s, F32) for s in shapes]
+        + [pltpu.SemaphoreType.DMA((2, len(OUTPUTS)))],
     )(*outs)
     return tuple(jnp.swapaxes(o, 1, 2) if i < 2 else o for i, o in enumerate(outs))
 

time: 202 us -> 147 us (0.73); the launches traced: 198 us -> 147 us
  Pallas kernels: 198 us -> 146 us
    pallas_call x1, Pallas kernels: 40.9 us -> 2.15 us  [per_device(): pl.pallas_call(write_out, out_shape=tuple((jax.ShapeDtypeStruct(s, F32) f...]
    pallas_call x1, Pallas kernels: 157 us -> 144 us  [per_device(): pl.pallas_call(body, out_shape=tuple((jax.ShapeDtypeStruct(s, F32) for s...]
where the time goes in v3:
time: 147 us
  Pallas kernels  146 us (99%)
    pallas_call x1, Pallas kernels, per_device(): pl.pallas_call(body, out_shape=tuple((jax.ShapeDtypeStruct(s, F32) for s...  144 us

profile of v3, /device:TPU:1, one launch (start us, length us, event | category | flops | bytes accessed | tf_op | source)
XLA Modules:
  0.0 147.2 jit_solution(4456014249525661197)
XLA Ops:
  0.6 144.2 %shard_map.172 = (f32[1,64,1024]{2,1,0:T(8,128)}, f32[1,64,768]{2,1,0:T(8,128)}, f32[1,96,512]{2,1,0:T(8,128)}, f32[1,512,128]{2,1,0:T(8,128)}, f32[1,384,128]{2,1,0:T(8,128)}, /*index=5*/f32[384,128]{1,0:T(8,128)}) custom-call(bf16[1,1024,512]{2,1,0:T(8,128)(2,1)} %refs_0_.1, bf16[1,256,1024]{2,1,0:T(8,128)(2,1)} %refs_1_.1, bf16[1,1536,384]{2,1,0:T(8,128)(2,1)} %refs_2_.1, ...), custom_call_target="tpu_custom_call" | custom-call | tf_op jit(solution)/shard_map/pallas_call | solution.py:805
  144.8 2.2 %shard_map.173 = (f32[1,64,1024]{2,1,0:T(8,128)}, f32[1,64,768]{2,1,0:T(8,128)}, f32[1,96,512]{2,1,0:T(8,128)}, f32[1,512,128]{2,1,0:T(8,128)}, f32[1,384,128]{2,1,0:T(8,128)}, /*index=5*/f32[384,128]{1,0:T(8,128)}) custom-call(f32[1,64,1024]{2,1,0:T(8,128)} %get-tuple-element.18.refs_0_, f32[1,64,768]{2,1,0:T(8,128)} %get-tuple-element.19.refs_1_, ...), custom_call_target="tpu_custom_call" | custom-call | tf_op jit(solution)/shard_map/pallas_call | solution.py:815

commit v4 on v3

--- a/solution.py
+++ b/solution.py
@@ -102,6 +102,7 @@
     b_vr=((2, 4, 256, 128), BF),
     b_vxs=((7, 256, 128), BF),
     b_vxr=((7, 256, 128), BF),
+    b_vo=((256, 128), BF),
     b_ck=((4, 256, 128), BF),
     b_ls=((4, 512, 128), BF),
     b_k=((4, 512, 128), F32),
@@ -115,7 +116,7 @@
     b_mr=((3, 512, 128), BF),
 )
 N_REMOTE = 320
-ORDER = "BFBFBFBFBBFFBFBBFBFBFFBBFBFFBFBBFBFBFFBBFBF"
+ORDER = "BFBFBFBFBBFFBFBBBFFBFFBBFBFFBBFBBFFBFBFBFBF"
 N_LOCAL = len(INPUTS) + len(OUTPUTS)
 
 
@@ -322,18 +323,25 @@
         for j in range(4):
             out[j] = r[:, j * 128 : (j + 1) * 128].astype(out.dtype)
 
-    def pick(matrix, vec, out, part):
+    def pick(matrix, vec, out, part, give):
         core = []
-        for q in range(2):
-
-            @pl.loop(0, 4)
-            def _(k):
-                at = pl.multiple_of(q * 2048 + k * 512, 512)
+        order = (1, 3, 2, 0)
+        for i, d in enumerate(order):
+            ch = (x + d) % 4
+
+            @pl.loop(0, 2)
+            def _(q):
+                at = pl.multiple_of(q * 2048 + ch * 512, 512)
                 r = dot_t(matrix[:, pl.ds(at, 512)], vec[...])
-                out[q, k] = r.astype(BF).reshape(2, 256, 128)
-
-            core.append(send(out.at[q, :, sib], part.at[q], sibling))
-        return core
+                out[q, ch] = r.astype(BF).reshape(2, 256, 128)
+
+            core.append(send(out.at[:, ch, sib], part.at[:, ch], sibling))
+            if i:
+                core[i - 1].wait_recv()
+                give(order[i - 1])
+        yield
+        core[3].wait_recv()
+        give(0)
 
     def hand_on(keep, part, buf, count):
         @tiles(count, 128 if count % 128 == 0 else 96)
@@ -504,7 +512,32 @@
         got = spread(v.f_rx.at[z], at_z)
         yield
         arrive(got)
-        core = []
+        core, got_a, got_b = [], [], []
+
+        def settle(i):
+            dy = (1, 3, 2, 0)[i]
+            s = (sec + dy) % 4
+            core[i].wait_recv()
+            if dy:
+
+                @pl.loop(0, 4)
+                def _(k):
+                    v.f_bs[dy - 1, k] = root_sum(s, k, 256).astype(BF)
+
+                got_b.append(send(v.f_bs.at[dy - 1], v.f_br.at[dy - 1], at_y(dy)))
+            else:
+
+                @pl.loop(0, 4)
+                def _(k):
+                    v.f_ob[k] = root_sum(s, k, 256)
+
+            part = []
+            for d in (1, 3, 2):
+                v.f_as[d - 1, s] = root_sum(s, (x + d) % 4, 0).astype(BF)
+                part.append(send(v.f_as.at[d - 1, s], v.f_ar.at[d - 1, s], at_x(d)))
+            got_a.append(part)
+            v.f_oa[s] = root_sum(s, x, 0)
+
         for dy in (1, 3, 2, 0):
             s = (sec + dy) % 4
 
@@ -518,30 +551,10 @@
                         v.f_t[cc, s, 2 * k + j] = r[at : at + 96].astype(BF)
 
             core.append(send(v.f_t.at[sib, s], v.f_tr.at[s], sibling))
-        yield
-        got_a, got_b = [], []
-        for i, dy in enumerate((1, 3, 2, 0)):
-            s = (sec + dy) % 4
-            core[i].wait_recv()
-            if dy:
-
-                @pl.loop(0, 4)
-                def _(k):
-                    v.f_bs[dy - 1, k] = root_sum(s, k, 256).astype(BF)
-
-                got_b.append(send(v.f_bs.at[dy - 1], v.f_br.at[dy - 1], at_y(dy)))
-            else:
-
-                @pl.loop(0, 4)
-                def _(k):
-                    v.f_ob[k] = root_sum(s, k, 256)
-
-            part = []
-            for d in (1, 3, 2):
-                v.f_as[d - 1, s] = root_sum(s, (x + d) % 4, 0).astype(BF)
-                part.append(send(v.f_as.at[d - 1, s], v.f_ar.at[d - 1, s], at_x(d)))
-            got_a.append(part)
-            v.f_oa[s] = root_sum(s, x, 0)
+            if len(core) > 1:
+                settle(len(core) - 2)
+        yield
+        settle(3)
         yield
 
         def gathered(total, part, k):
@@ -621,27 +634,39 @@
             v.b_rx[m, :] = own.astype(BF)
 
         emit(v.o_rx, 5)
-        core = pick(v.rsel, v.b_rx, v.b_t, v.b_tr)
-        yield
-        arrive(core)
-        got = []
-        for d in (1, 3, 2):
+        halves = (pl.ds(0, 128), pl.ds(128, 128))
+        got = ([], [])
+
+        def give(d):
             ch = (x + d) % 4
             for q in range(2):
-                v.b_txs[d - 1, q] = v.b_t[q, ch, c] + v.b_tr[q, ch]
-            got.append(send(v.b_txs.at[d - 1], v.b_txr.at[d - 1], at_x(d)))
-        yield
-        arrive(got)
-        for q in range(2):
-            own = v.b_t[q, x, c] + v.b_tr[q, x]
-            v.b_tp[q] = own + ((v.b_txr[0, q] + v.b_txr[1, q]) + v.b_txr[2, q])
+                own = v.b_t[q, ch, c] + v.b_tr[q, ch]
+                if d:
+                    v.b_txs[d - 1, q] = own
+                else:
+                    v.b_tp[q] = own
+            for half, at in enumerate(halves if d else ()):
+                src, dst = v.b_txs.at[d - 1, :, at], v.b_txr.at[d - 1, :, at]
+                got[half].append(send(src, dst, at_x(d)))
+
+        yield from pick(v.rsel, v.b_rx, v.b_t, v.b_tr, give)
+        yield
+        got_y = ([], [])
+        for half, at in enumerate(halves):
+            arrive(got[half])
+            for q in range(2):
+                found = (v.b_txr[0, q, at] + v.b_txr[1, q, at]) + v.b_txr[2, q, at]
+                v.b_tp[q, at] = v.b_tp[q, at] + found
+            for d in (1, 3, 2):
+                src = v.b_tp.at[((sec + d) % 4) // 2, at]
+                got_y[half].append(send(src, v.b_tpr.at[d - 1, at], at_y(d)))
+        yield
         got = []
-        for d in (1, 3, 2):
-            got.append(send(v.b_tp.at[((sec + d) % 4) // 2], v.b_tpr.at[d - 1], at_y(d)))
-        yield
-        arrive(got)
-        v.b_pk[z] = v.b_tp[p] + ((v.b_tpr[0] + v.b_tpr[1]) + v.b_tpr[2])
-        got = spread(v.b_pk.at[z], at_z)
+        for half, at in enumerate(halves):
+            arrive(got_y[half])
+            found = (v.b_tpr[0, at] + v.b_tpr[1, at]) + v.b_tpr[2, at]
+            v.b_pk[z, at] = v.b_tp[p, at] + found
+            got += spread(v.b_pk.at[z, at], at_z)
         yield
         need(v.wpl)
         arrive(got)
@@ -693,21 +718,32 @@
 
         emit(v.o_px, 4)
         v.b_fx[384:, :] = v.b_pk[z, pl.ds(h * 128, 128), :]
-        core = pick(v.sel, v.b_fx, v.b_v, v.b_vr)
-        yield
-        arrive(core)
-        got = []
-        for d, q in eight[1:] + eight[:1]:
+        got = ([], [])
+
+        def give(d):
             ch = (x + d) % 4
-            a = oh if q else h
-            v.b_vxs[slot(d, q)] = v.b_v[a, ch, c] + v.b_vr[a, ch]
-            got.append(send(v.b_vxs.at[slot(d, q)], v.b_vxr.at[slot(d, q)], at_px(d, q)))
-        yield
-        arrive(got)
-        own = v.b_v[h, x, c] + v.b_vr[h, x] + (v.b_vxr[0] + v.b_vxr[1] + v.b_vxr[2])
-        own = own + ((v.b_vxr[3] + v.b_vxr[4]) + (v.b_vxr[5] + v.b_vxr[6]))
-        v.b_ck[z] = own
-        got = spread(v.b_ck.at[z], at_z)
+            for q in (0, 1):
+                a = oh if q else h
+                own = v.b_v[a, ch, c] + v.b_vr[a, ch]
+                if d or q:
+                    v.b_vxs[slot(d, q)] = own
+                else:
+                    v.b_vo[...] = own
+            for half, at in enumerate(halves):
+                for q in (0, 1) if d else (1,):
+                    src, dst = v.b_vxs.at[slot(d, q), at], v.b_vxr.at[slot(d, q), at]
+                    got[half].append(send(src, dst, at_px(d, q)))
+
+        yield from pick(v.sel, v.b_fx, v.b_v, v.b_vr, give)
+        yield
+        spreads = []
+        for half, at in enumerate(halves):
+            arrive(got[half])
+            own = v.b_vo[at] + ((v.b_vxr[0, at] + v.b_vxr[1, at]) + v.b_vxr[2, at])
+            own = own + (v.b_vxr[3, at] + v.b_vxr[4, at])
+            v.b_ck[z, at] = own + (v.b_vxr[5, at] + v.b_vxr[6, at])
+            spreads += spread(v.b_ck.at[z, at], at_z)
+        got = spreads
         yield
         need(v.wcl)
         arrive(got)

time: 147 us -> 138 us (0.939)
  Pallas kernels: 146 us -> 137 us
    pallas_call x1, Pallas kernels: 144 us -> 135 us  [per_device(): pl.pallas_call(body, out_shape=tuple((jax.ShapeDtypeStruct(s, F32) for s...]
where the time goes in v4:
time: 138 us
  Pallas kernels  137 us (99%)
    pallas_call x1, Pallas kernels, per_device(): pl.pallas_call(body, out_shape=tuple((jax.ShapeDtypeStruct(s, F32) for s...  135 us

profile of v4, /device:TPU:1, one launch (start us, length us, event | category | flops | bytes accessed | tf_op | source)
XLA Modules:
  0.0 137.9 jit_solution(11556575932350234069)
XLA Ops:
  0.6 134.9 %shard_map.172 = (f32[1,64,1024]{2,1,0:T(8,128)}, f32[1,64,768]{2,1,0:T(8,128)}, f32[1,96,512]{2,1,0:T(8,128)}, f32[1,512,128]{2,1,0:T(8,128)}, f32[1,384,128]{2,1,0:T(8,128)}, /*index=5*/f32[384,128]{1,0:T(8,128)}) custom-call(bf16[1,1024,512]{2,1,0:T(8,128)(2,1)} %refs_0_.1, bf16[1,256,1024]{2,1,0:T(8,128)(2,1)} %refs_1_.1, bf16[1,1536,384]{2,1,0:T(8,128)(2,1)} %refs_2_.1, ...), custom_call_target="tpu_custom_call" | custom-call | tf_op jit(solution)/shard_map/pallas_call | solution.py:841
  135.5 2.2 %shard_map.173 = (f32[1,64,1024]{2,1,0:T(8,128)}, f32[1,64,768]{2,1,0:T(8,128)}, f32[1,96,512]{2,1,0:T(8,128)}, f32[1,512,128]{2,1,0:T(8,128)}, f32[1,384,128]{2,1,0:T(8,128)}, /*index=5*/f32[384,128]{1,0:T(8,128)}) custom-call(f32[1,64,1024]{2,1,0:T(8,128)} %get-tuple-element.18.refs_0_, f32[1,64,768]{2,1,0:T(8,128)} %get-tuple-element.19.refs_1_, ...), custom_call_target="tpu_custom_call" | custom-call | tf_op jit(solution)/shard_map/pallas_call | solution.py:851
